TPU v7x, 512 devices: a whole 4x8x8 slice. The times are simulated.
512 devices in a mesh: gx: 16 (over z_lo, x), gy: 32 (over y, z_hi, core).
Axes of the slice: x: 4, y: 8, z: 8 (z_hi: 2, z_lo: 4; z = z_hi * 4 + z_lo), core: 2. Of those that a mesh axis runs over, the one named last changes fastest.
Arguments:
- estimate: float32 [8, 2048, 4096], P(None, 'gy', 'gx'), may hold values from 0.5 to 2
- views: float32 [4, 8, 2048, 4096], P(None, None, 'gy', 'gx'), may hold values from 0.25 to 4
- psf_x: float32 [4, 15], replicated, may hold values from 0.05 to 1
- psf_y: float32 [4, 15], replicated, may hold values from 0.05 to 1
- psf_z: float32 [4, 15], replicated, may hold values from 0.05 to 1
- block_offsets: int32 [4, 2, 32, 16], replicated, may hold values from -15 to 15
- sub_shifts: int32 [4, 3, 32, 16], replicated, may hold values from 0 to 3
Outputs:
- estimate_next: float32 [8, 2048, 4096], P(None, 'gy', 'gx')
All inputs are finite; a program needn't handle non-finite values.
Results may differ from a plain program's by a relative error of at most 0.0003.
Values sent between devices are 32-bit elements; how exact they have to be, the bound alone decides.
No kernel may reach another device: no remote copies, remote signals or barrier semaphores. Data moves between devices by JAX's collectives and lax.ppermute only.
A program may use at most 64 MiB of HBM per device.

v0:
```python
import functools

import jax
import jax.numpy as jnp
from jax import lax
from jax.experimental import pallas as pl
from jax.experimental.pallas import tpu as pltpu
from jax.sharding import PartitionSpec as P

F32 = jnp.float32
BF16 = jnp.bfloat16
VIEWS = 4
TAPS = 15
Z = 8
ROWS = 64
COLS = 256
SET = 48
EDGE = 24

SMEM = pl.BlockSpec(memory_space=pltpu.SMEM)
VMEM = pl.BlockSpec(memory_space=pltpu.VMEM)


def iota(shape, dim):
    return lax.broadcasted_iota(jnp.int32, shape, dim)


def sample_row(inner, idx):
    if inner:
        return idx + 8
    return jnp.where(
        idx < 8, idx, jnp.where(idx < 16, idx + 48, jnp.where(idx < 32, idx - 32, idx + 32))
    )


def estimate_row(inner, idx):
    return idx if inner else jnp.where(idx < 40, idx - 24, idx + 8)


def output_row(inner, idx):
    return idx if inner else jnp.where(idx < 64, idx, jnp.where(idx < 88, idx - 88, idx - 24))


def estimate_rows(inner):
    return 64 if inner else 80


def output_rows(inner):
    return 64 if inner else 112


def strip_col(lane):
    return jnp.where(lane < 8, lane - 8, jnp.where(lane < 16, lane + 248, 4096))


def split(value):
    high = value.astype(BF16)
    return high, (value - high.astype(F32)).astype(BF16)


def band(k_ref, base, differ):
    total = jnp.zeros(differ.shape, F32)
    for tap in range(TAPS):
        total = jnp.where(differ == tap, k_ref[base + tap], total)
    return total


def matrices_kernel(k_ref, ly_i, ly_o, f_hi, f_lo, f_t, f_s, b_hi, b_lo, b_t, m_i, n_i, m_o, n_o):
    kx, ky = 0, VIEWS * TAPS
    for inner, ly in ((True, ly_i), (False, ly_o)):
        count = estimate_rows(inner)
        shape = (SET, 3 * count)
        lane = iota(shape, 1)
        seg = jnp.where(lane < count, 0, jnp.where(lane < 2 * count, 1, 2))
        differ = estimate_row(inner, lane - seg * count) - sample_row(inner, iota(shape, 0)) + 7
        for v in range(VIEWS):
            weight = band(k_ref, ky + v * TAPS, differ)
            high = weight.astype(BF16).astype(F32)
            ly[v * SET : (v + 1) * SET, :] = jnp.where(seg < 2, high, weight - high).astype(BF16)

    for inner, m_ref, n_ref in ((True, m_i, n_i), (False, m_o, n_o)):
        shape = (output_rows(inner), VIEWS * SET)
        lane = iota(shape, 1)
        view = lane // SET
        differ = output_row(inner, iota(shape, 0)) - sample_row(inner, lane - view * SET) + 7
        weight = jnp.zeros(shape, F32)
        for v in range(VIEWS):
            weight = jnp.where(view == v, band(k_ref, ky + v * TAPS, differ), weight)
        high, low = split(weight)
        m_ref[...] = high
        n_ref[...] = low

    def per_view(v, carry):
        base = kx + v * TAPS
        differ = iota((COLS, COLS), 0) - iota((COLS, COLS), 1) + 7
        high, low = split(band(k_ref, base, differ))
        f_hi[v] = high
        f_lo[v] = low
        high, low = split(band(k_ref, base, 14 - differ))
        b_hi[v] = high
        b_lo[v] = low
        for out_ref, width in ((f_t, COLS), (f_s, 128)):
            shape = (256, width)
            row = iota(shape, 0)
            second = row >= 128
            h = jnp.where(second, row - 128, row)
            place = jnp.where(h < 48, h, h - 48)
            source = jnp.where(
                place < 16,
                place - 16,
                jnp.where(place < 32, place + 240, jnp.where(place < 40, place - 32, place + 208)),
            )
            limit = 32 if width == COLS else 48
            good = (place < limit) & (h < jnp.where(second, 48, 96))
            target = iota(shape, 1) if width == COLS else strip_col(iota(shape, 1))
            weight = band(k_ref, base, jnp.where(good, source - target + 7, -1))
            high = weight.astype(BF16).astype(F32)
            out_ref[v] = jnp.where(second, weight - high, high).astype(BF16)
        shape = (128, COLS)
        row = iota(shape, 0)
        seg = row // 16
        differ = iota(shape, 1) - strip_col(row - seg * 16) + 7
        weight = band(k_ref, base, jnp.where(seg < 3, differ, -1))
        high = weight.astype(BF16).astype(F32)
        b_t[v] = jnp.where(seg < 2, high, weight - high).astype(BF16)
        return carry

    lax.fori_loop(0, VIEWS, per_view, 0)


def matrices(kernels):
    shapes = [
        (192, 192), (192, 240), (4, 256, 256), (4, 256, 256), (4, 256, 256), (4, 256, 128),
        (4, 256, 256), (4, 256, 256), (4, 128, 256), (64, 192), (64, 192), (112, 192), (112, 192),
    ]
    return pl.pallas_call(
        matrices_kernel,
        out_shape=[jax.ShapeDtypeStruct(s, BF16) for s in shapes],
        in_specs=[SMEM],
        out_specs=[VMEM] * len(shapes),
        name="matrices",
        cost_estimate=pl.CostEstimate(flops=8_000_000, bytes_accessed=4_000_000, transcendentals=0),
    )(kernels)


def pack_estimate_kernel(e_ref, left_ref, right_ref):
    lane = iota((ROWS, 128), 1) // 16
    left = jnp.zeros((ROWS, 128), F32)
    right = jnp.zeros((ROWS, 128), F32)
    for z in range(Z):
        a = pltpu.roll(e_ref[z, :, 0:128], z * 16, 1) if z else e_ref[z, :, 0:128]
        b = pltpu.roll(e_ref[z, :, 128:256], (z * 16 + 16) % 128, 1) if z < 7 else e_ref[z, :, 128:256]
        left = jnp.where(lane == z, a, left)
        right = jnp.where(lane == z, b, right)
    left_ref[...] = left
    right_ref[...] = right


def pack_estimate(estimate):
    return pl.pallas_call(
        pack_estimate_kernel,
        out_shape=[jax.ShapeDtypeStruct((ROWS, 128), F32)] * 2,
        in_specs=[VMEM],
        out_specs=[VMEM] * 2,
        name="pack_estimate",
    )(estimate)


def pack_views_kernel(v_ref, left_ref, right_ref):
    lane = iota((ROWS, 128), 1) // 24
    for v in range(VIEWS):
        for half in range(2):
            left = jnp.zeros((ROWS, 128), F32)
            right = jnp.zeros((ROWS, 128), F32)
            for q in range(4):
                z = half * 4 + q
                a = v_ref[v, z, :, 0:128]
                a = pltpu.roll(a, q * 24, 1) if q else a
                b = pltpu.roll(v_ref[v, z, :, 128:256], q * 24 + 24, 1)
                left = jnp.where(lane == q, a, left)
                right = jnp.where(lane == q, b, right)
            left_ref[v, :, half * 128 : half * 128 + 128] = left
            right_ref[v, :, half * 128 : half * 128 + 128] = right


def pack_views(views):
    return pl.pallas_call(
        pack_views_kernel,
        out_shape=[jax.ShapeDtypeStruct((VIEWS, ROWS, COLS), F32)] * 2,
        in_specs=[VMEM],
        out_specs=[VMEM] * 2,
        name="pack_views",
        cost_estimate=pl.CostEstimate(flops=1_000_000, bytes_accessed=2_600_000, transcendentals=0),
    )(views)


def pack_rows_kernel(e_ref, l_ref, r_ref, first_ref, last_ref):
    for out_ref, start in ((first_ref, 0), (last_ref, ROWS - EDGE)):
        for z in range(Z):
            out_ref[z * EDGE : (z + 1) * EDGE, :] = e_ref[z, start : start + EDGE, :]
        out_ref[Z * EDGE :, 0:128] = l_ref[start : start + EDGE, :]
        out_ref[Z * EDGE :, 128:256] = r_ref[start : start + EDGE, :]


def pack_rows(estimate, left, right):
    return pl.pallas_call(
        pack_rows_kernel,
        out_shape=[jax.ShapeDtypeStruct(((Z + 1) * EDGE, COLS), F32)] * 2,
        in_specs=[VMEM] * 3,
        out_specs=[VMEM] * 2,
        name="pack_rows",
    )(estimate, left, right)


def warp_kernel(p_ref, v_ref, l_ref, r_ref, wi_ref, si_ref, wo_ref, so_ref,
                src, c_hi, c_lo, s_hi, s_lo):
    v = pl.program_id(0)
    j, i = p_ref[180], p_ref[181]
    lane = iota((ROWS, 128), 1)
    for z in range(Z):
        q, half = z % 4, z // 4
        a, b = v_ref[0, z, :, 0:128], v_ref[0, z, :, 128:256]
        left = l_ref[0, :, half * 128 : half * 128 + 128]
        right = r_ref[0, :, half * 128 : half * 128 + 128]
        left = pltpu.roll(left, (128 - q * 24) % 128, 1) if q else left
        right = pltpu.roll(right, (128 + 24 - q * 24) % 128, 1) if q != 1 else right
        edge = jnp.where(lane < 24, left, jnp.where(lane < 48, right, jnp.where(
            lane < 64, pltpu.roll(a, 48, 1), jnp.where(lane < 80, pltpu.roll(b, 80, 1), 0.0))))
        for t, part in enumerate((a, b, edge)):
            high, low = split(part)
            src[z * 128 : z * 128 + 64, t * 128 : t * 128 + 128] = high
            src[z * 128 + 64 : z * 128 + 128, t * 128 : t * 128 + 128] = low
    src[Z * 128 :, :] = jnp.zeros((128, 384), BF16)

    def offset(axis, b, c):
        return p_ref[((v * 2 + axis) * 3 + b) * 3 + c]

    def quarter(axis, b, c):
        return p_ref[72 + ((v * 3 + axis) * 3 + b) * 3 + c].astype(F32) * 0.25

    shape = (96, 256)
    row = iota(shape, 0)
    source = iota(shape, 1)
    upper_plane = source >= 128
    source = source & 63
    target = jnp.where(row < 48, row + 8, jnp.where(row < 56, row - 48, jnp.where(
        row < 64, row, jnp.where(row < 80, row - 80, row - 16))))

    def rows_matrix(c):
        def pick(values):
            return jnp.where(row < 64, values[1], jnp.where(row < 80, values[0], values[2]))

        good_c = (i > 0) if c == 0 else ((i < p_ref[183]) if c == 2 else (i >= 0))
        good = [((j > 0) & good_c).astype(F32), good_c.astype(F32), ((j < p_ref[182]) & good_c).astype(F32)]
        shift = pick([offset(1, b, c) for b in range(3)])
        f_y = pick([quarter(1, b, c) for b in range(3)])
        f_z0 = pick([(1.0 - quarter(2, b, c)) * good[b] for b in range(3)])
        f_z1 = pick([quarter(2, b, c) * good[b] for b in range(3)])
        tap = source - target - shift
        weight = jnp.where(tap == 0, 1.0 - f_y, jnp.where(tap == 1, f_y, 0.0))
        return (weight * jnp.where(upper_plane, f_z1, f_z0)).astype(BF16)

    center = rows_matrix(1)
    sides = jnp.concatenate([rows_matrix(0), rows_matrix(2)], axis=0)
    for z in range(Z):
        data = src[z * 128 : z * 128 + 256, :]
        c = jnp.dot(center, data, preferred_element_type=F32)
        s = jnp.dot(sides, data[:, 256:384], preferred_element_type=F32)
        for value, hi_ref, lo_ref, col, width in (
            (c, c_hi, c_lo, 0, 384), (s[0:96], s_hi, s_lo, 0, 128), (s[96:192], s_hi, s_lo, 128, 128)):
            high, low = split(value)
            for ref, part in ((hi_ref, high), (lo_ref, low)):
                ref[z * 64 : z * 64 + 64, col : col + width] = part[0:64]
                ref[512 + z * 16 : 528 + z * 16, col : col + width] = part[64:80]
                ref[640 + z * 16 : 656 + z * 16, col : col + width] = part[80:96]

    for b, start, count in ((1, 0, 512), (0, 512, 128), (2, 640, 128)):
        k = iota((384, COLS), 0)
        col = jnp.where(k < 256, k, jnp.where(k < 280, k - 280, jnp.where(k < 304, k - 24, 8192)))
        tap = col - iota((384, COLS), 1) - offset(0, b, 1)
        f_x = quarter(0, b, 1)
        x_map = jnp.where(tap == 0, 1.0 - f_x, jnp.where(tap == 1, f_x, 0.0)).astype(BF16)
        k = iota((256, 128), 0)
        is_right = k >= 128
        h = k & 127
        col = jnp.where(h < 24, h - 24, jnp.where(h < 48, h + 232, jnp.where(
            h < 64, h - 48, jnp.where(h < 80, h + 176, 8192))))
        out_lane = iota((256, 128), 1)
        right_lane = out_lane >= 8
        tap = col - strip_col(out_lane) - jnp.where(is_right, offset(0, b, 2), offset(0, b, 0))
        tap = jnp.where(is_right == right_lane, tap, -1)
        f_x = jnp.where(is_right, quarter(0, b, 2), quarter(0, b, 0))
        s_map = jnp.where(tap == 0, 1.0 - f_x, jnp.where(tap == 1, f_x, 0.0)).astype(BF16)
        rows = slice(start, start + count)
        w = jnp.dot(c_hi[rows], x_map, preferred_element_type=F32)
        w += jnp.dot(c_lo[rows], x_map, preferred_element_type=F32)
        s = jnp.dot(s_hi[rows], s_map, preferred_element_type=F32)
        s += jnp.dot(s_lo[rows], s_map, preferred_element_type=F32)
        for value, i_ref, o_ref in ((w, wi_ref, wo_ref), (s, si_ref, so_ref)):
            for z in range(Z):
                if b == 1:
                    i_ref[0, z] = value[z * 64 : z * 64 + 48]
                    o_ref[0, z, 0:16] = value[z * 64 + 48 : z * 64 + 64]
                else:
                    at = 16 if b == 0 else 32
                    o_ref[0, z, at : at + 16] = value[z * 16 : z * 16 + 16]


def warp(params, views, left, right):
    w = jax.ShapeDtypeStruct((VIEWS, Z, SET, COLS), F32)
    s = jax.ShapeDtypeStruct((VIEWS, Z, SET, 128), F32)
    w_spec = pl.BlockSpec((1, Z, SET, COLS), lambda v: (v, 0, 0, 0))
    s_spec = pl.BlockSpec((1, Z, SET, 128), lambda v: (v, 0, 0, 0))
    side = pl.BlockSpec((1, ROWS, COLS), lambda v: (v, 0, 0))
    return pl.pallas_call(
        warp_kernel,
        grid=(VIEWS,),
        out_shape=[w, s, w, s],
        in_specs=[SMEM, pl.BlockSpec((1, Z, ROWS, COLS), lambda v: (v, 0, 0, 0)), side, side],
        out_specs=[w_spec, s_spec, w_spec, s_spec],
        scratch_shapes=[
            pltpu.VMEM((9 * 128, 384), BF16),
            pltpu.VMEM((768, 384), BF16),
            pltpu.VMEM((768, 384), BF16),
            pltpu.VMEM((768, 256), BF16),
            pltpu.VMEM((768, 256), BF16),
        ],
        name="warp",
        cost_estimate=pl.CostEstimate(flops=6_000_000_000, bytes_accessed=8_000_000, transcendentals=0),
    )(params, views, left, right)


def main_kernel(inner, *refs):
    refs = list(refs)
    k_ref, e_ref, l_ref, r_ref = refs[:4]
    refs = refs[4:]
    if not inner:
        above, below = refs[:2]
        refs = refs[2:]
    w_ref, s_ref, ly, f_hi, f_lo, f_t, f_s, b_hi, b_lo, b_t, m_ref, n_ref = refs[:12]
    refs = refs[12:]
    if inner:
        out_refs, refs = refs[:1], refs[1:]
    else:
        partial_ref, out_refs, refs = refs[0], refs[1:4], refs[4:]
    d, g_hi, g_lo, g_t, cen, stp, q_hi, q_lo, q_t, x2 = refs
    count = estimate_rows(inner)
    lane = iota((count, 128), 1)
    lane_out = iota((VIEWS * SET, 128), 1)
    for z in range(Z):
        if inner:
            c0, c1 = e_ref[z, :, 0:128], e_ref[z, :, 128:256]
            lh, rh = l_ref[...], r_ref[...]
        else:
            edge = slice(z * EDGE, (z + 1) * EDGE)
            tail = slice(Z * EDGE, (Z + 1) * EDGE)

            def rows(cols, own):
                return jnp.concatenate(
                    [above[edge, cols], own[0:16], own[48:64], below[edge, cols]], axis=0)

            c0 = rows(slice(0, 128), e_ref[z, :, 0:128])
            c1 = rows(slice(128, 256), e_ref[z, :, 128:256])
            lh = jnp.concatenate(
                [above[tail, 0:128], l_ref[0:16], l_ref[48:64], below[tail, 0:128]], axis=0)
            rh = jnp.concatenate(
                [above[tail, 128:256], r_ref[0:16], r_ref[48:64], below[tail, 128:256]], axis=0)
        lh = pltpu.roll(lh, (128 - z * 16) % 128, 1) if z else lh
        rh = pltpu.roll(rh, (128 + 16 - z * 16) % 128, 1) if z != 1 else rh
        h = jnp.where(lane < 16, lh, jnp.where(lane < 32, rh, jnp.where(
            lane < 40, pltpu.roll(c0, 32, 1), jnp.where(lane < 48, pltpu.roll(c1, 48, 1), 0.0))))
        h = jnp.where(lane < 48, h, jnp.where(lane < 96, pltpu.roll(h, 48, 1), 0.0))
        for t, part in enumerate((c0, c1, h)):
            high, low = split(part)
            cols = slice(t * 128, t * 128 + 128)
            d[0:count, cols] = high
            d[count : 2 * count, cols] = low
            d[2 * count : 3 * count, cols] = high
        y = jnp.dot(ly[...], d[...], preferred_element_type=F32)
        high = y.astype(BF16)
        low = y - high.astype(F32)
        both = jnp.where(lane_out < 48, y[:, 256:384], low[:, 256:384]).astype(BF16)
        low = low.astype(BF16)
        for v in range(VIEWS):
            to, at = slice(z * SET, (z + 1) * SET), slice(v * SET, (v + 1) * SET)
            g_hi[v, to, :] = high[at, 0:256]
            g_lo[v, to, :] = low[at, 0:256]
            g_t[v, to, 0:128] = both[at]
            g_t[v, to, 128:256] = high[at, 256:384]

    def per_view(v, carry):
        def dot(a, b):
            return jnp.dot(a, b, preferred_element_type=F32)

        cen[...] = (dot(g_hi[v], f_hi[v]) + dot(g_lo[v], f_hi[v])) + (
            dot(g_hi[v], f_lo[v]) + dot(g_t[v], f_t[v]))
        stp[...] = dot(g_t[v], f_s[v])
        taps = [k_ref[2 * VIEWS * TAPS + v * TAPS + t] for t in range(TAPS)]
        for rb in range(3):
            for t in range(3):
                ref, cols = (cen, slice(t * 128, t * 128 + 128)) if t < 2 else (stp, slice(0, 128))
                at = [slice(z * SET + rb * 16, z * SET + rb * 16 + 16) for z in range(Z)]
                f = [ref[at[z], cols] for z in range(Z)]
                ratio = []
                for z in range(Z):
                    total = taps[7 - z] * f[0]
                    for y in range(1, Z):
                        total = total + taps[y - z + 7] * f[y]
                    total = jnp.where(total == 0.0, 1.0, total)
                    rows = slice(rb * 16, rb * 16 + 16)
                    top = w_ref[v, z, rows, cols] if t < 2 else s_ref[v, z, rows, cols]
                    ratio.append(top / total)
                for z in range(Z):
                    total = taps[z + 7] * ratio[0]
                    for y in range(1, Z):
                        total = total + taps[z - y + 7] * ratio[y]
                    if t < 2:
                        high, low = split(total)
                        q_hi[at[z], cols] = high
                        q_lo[at[z], cols] = low
                    else:
                        high = total.astype(BF16).astype(F32)
                        low = total - high
                        lanes = iota((16, 128), 1)
                        q_t[at[z], :] = jnp.where(lanes < 16, high, jnp.where(
                            lanes < 32, pltpu.roll(low, 16, 1), jnp.where(
                                lanes < 48, pltpu.roll(high, 32, 1), 0.0))).astype(BF16)
        x = (dot(q_hi[...], b_hi[v]) + dot(q_lo[...], b_hi[v])) + (
            dot(q_hi[...], b_lo[v]) + dot(q_t[...], b_t[v]))
        high, low = split(x)
        for z in range(Z):
            x2[z, 0, v] = high[z * SET : (z + 1) * SET]
            x2[z, 1, v] = low[z * SET : (z + 1) * SET]
        return carry

    lax.fori_loop(0, VIEWS, per_view, 0)
    for z in range(Z):
        high = x2[z, 0].reshape(VIEWS * SET, COLS)
        low = x2[z, 1].reshape(VIEWS * SET, COLS)
        out = jnp.dot(m_ref[...], high, preferred_element_type=F32)
        out += jnp.dot(m_ref[...], low, preferred_element_type=F32)
        out += jnp.dot(n_ref[...], high, preferred_element_type=F32)
        if inner:
            out_refs[0][z] = out
        else:
            out_refs[0][z] = out[0:64] + partial_ref[z]
            out_refs[1][z] = out[64:88]
            out_refs[2][z] = out[88:112]


def main(inner, *args):
    own = jax.ShapeDtypeStruct((Z, ROWS, COLS), F32)
    edge = jax.ShapeDtypeStruct((Z, EDGE, COLS), F32)
    rows = Z * SET
    return pl.pallas_call(
        functools.partial(main_kernel, inner),
        out_shape=[own] if inner else [own, edge, edge],
        in_specs=[SMEM] + [VMEM] * (len(args) - 1),
        out_specs=[VMEM] * (1 if inner else 3),
        scratch_shapes=[
            pltpu.VMEM((3 * estimate_rows(inner), 384), BF16),
            pltpu.VMEM((VIEWS, rows, 256), BF16),
            pltpu.VMEM((VIEWS, rows, 256), BF16),
            pltpu.VMEM((VIEWS, rows, 256), BF16),
            pltpu.VMEM((rows, 256), F32),
            pltpu.VMEM((rows, 128), F32),
            pltpu.VMEM((rows, 256), BF16),
            pltpu.VMEM((rows, 256), BF16),
            pltpu.VMEM((rows, 128), BF16),
            pltpu.VMEM((Z, 2, VIEWS, SET, COLS), BF16),
        ],
        name="inner_rows" if inner else "edge_rows",
        cost_estimate=pl.CostEstimate(flops=6_000_000_000, bytes_accessed=12_000_000, transcendentals=0),
    )(*args)


def final_kernel(e_ref, own_ref, up_ref, down_ref, out_ref):
    for z in range(Z):
        out_ref[z, 0:24] = e_ref[z, 0:24] * ((own_ref[z, 0:24] + up_ref[z]) * 0.25)
        out_ref[z, 24:40] = e_ref[z, 24:40] * (own_ref[z, 24:40] * 0.25)
        out_ref[z, 40:64] = e_ref[z, 40:64] * ((own_ref[z, 40:64] + down_ref[z]) * 0.25)


def final(*args):
    return pl.pallas_call(
        final_kernel,
        out_shape=jax.ShapeDtypeStruct((Z, ROWS, COLS), F32),
        in_specs=[VMEM] * 4,
        out_specs=VMEM,
        name="final",
    )(*args)


def shifted(first, last, axis):
    count = lax.axis_size(axis)
    up = [(i, i + 1) for i in range(count - 1)]
    down = [(i + 1, i) for i in range(count - 1)]
    return lax.ppermute(last, axis, up), lax.ppermute(first, axis, down)


def neighbours(table, j, i):
    padded = jnp.pad(table, ((0, 0), (0, 0), (1, 1), (1, 1)))
    zero = jnp.int32(0)
    return lax.dynamic_slice(padded, (zero, zero, j, i), table.shape[:2] + (3, 3)).reshape(-1)


def on_device(estimate, views, psf_x, psf_y, psf_z, block_offsets, sub_shifts):
    i, j = lax.axis_index("gx"), lax.axis_index("gy")
    psf = jnp.concatenate([psf_x, psf_y, psf_z], axis=0)
    kernels = (psf / jnp.sum(psf, axis=-1, keepdims=True)).reshape(-1)
    params = jnp.concatenate(
        [neighbours(block_offsets, j, i), neighbours(sub_shifts, j, i), j[None], i[None],
         jnp.array([lax.axis_size("gy") - 1, lax.axis_size("gx") - 1], jnp.int32)])
    e_left, e_right = shifted(*pack_estimate(estimate), "gx")
    mats = matrices(kernels)
    ly_i, ly_o, *x_mats, m_i, n_i, m_o, n_o = mats
    above, below = shifted(*pack_rows(estimate, e_left, e_right), "gy")
    v_left, v_right = shifted(*pack_views(views), "gx")
    w_i, s_i, w_o, s_o = warp(params, views, v_left, v_right)
    (inside,) = main(True, kernels, estimate, e_left, e_right, w_i, s_i, ly_i, *x_mats, m_i, n_i)
    own, up, down = main(
        False, kernels, estimate, e_left, e_right, above, below, w_o, s_o, ly_o, *x_mats,
        m_o, n_o, inside)
    from_above, from_below = shifted(up, down, "gy")
    return final(estimate, own, from_above, from_below)


def solution(mesh):
    in_specs = (P(None, "gy", "gx"), P(None, None, "gy", "gx"), P(), P(), P(), P(), P())
    out_specs = P(None, "gy", "gx")
    return jax.shard_map(
        on_device, mesh=mesh, in_specs=in_specs, out_specs=out_specs, check_vma=False
    )
```

profile of v0, /device:TPU:89, one launch (start us, length us, event | category | flops | bytes accessed | tf_op | source)
XLA Modules:
  0.0 103.1 jit_solution(18257617966487171458)
XLA Ops:
  0.0 3.0 %pack_views.1 = (f32[4,64,256]{2,1,0:T(8,128)}, f32[4,64,256]{2,1,0:T(8,128)}) custom-call(f32[4,8,64,256]{3,2,1,0:T(8,128)} %v_ref.3), custom_call_target="tpu_custom_call" | custom-call | flops 1000000 | bytes 2600000 | tf_op jit(solution)/shard_map/pack_views/pallas_call | solution.py:187
  3.0 3.1 %collective-permute-start.4 = (f32[4,64,256]{2,1,0:T(8,128)}, f32[4,64,256]{2,1,0:T(8,128)S(1)}, u32[]{:S(2)}, u32[]{:S(2)}) collective-permute-start(f32[4,64,256]{2,1,0:T(8,128)} %get-tuple-element.35), channel_id=1, source_target_pairs={{0,32},{32,64},{64,96},{96,128},{128,160},{160,192},{192,224},{224... | collective-permute-start | bytes 786440 | tf_op jit(solution)/shard_map/ppermute | solution.py:498
  6.2 4.3 %collective-permute-start.5 = (f32[4,64,256]{2,1,0:T(8,128)}, f32[4,64,256]{2,1,0:T(8,128)S(1)}, u32[]{:S(2)}, u32[]{:S(2)}) collective-permute-start(f32[4,64,256]{2,1,0:T(8,128)} %get-tuple-element.36), channel_id=1, source_target_pairs={{32,0},{64,32},{96,64},{128,96},{160,128},{192,160},{224,192},{256... | collective-permute-start | bytes 786440 | tf_op jit(solution)/shard_map/ppermute | solution.py:498
  10.4 1.8 %pack_estimate.1 = (f32[64,128]{1,0:T(8,128)}, f32[64,128]{1,0:T(8,128)}) custom-call(f32[8,64,256]{2,1,0:T(8,128)} %e_ref.5), custom_call_target="tpu_custom_call" | custom-call | tf_op jit(solution)/shard_map/pack_estimate/pallas_call | solution.py:160
  12.3 1.9 %collective-permute-start = (f32[64,128]{1,0:T(8,128)}, f32[64,128]{1,0:T(8,128)S(1)}, u32[]{:S(2)}, u32[]{:S(2)}) collective-permute-start(f32[64,128]{1,0:T(8,128)} %get-tuple-element.31), channel_id=1, source_target_pairs={{0,32},{32,64},{64,96},{96,128},{128,160},{160,192},{192,224},{224... | collective-permute-start | bytes 98312 | tf_op jit(solution)/shard_map/ppermute | solution.py:498
  14.2 5.5 %collective-permute-start.1 = (f32[64,128]{1,0:T(8,128)}, f32[64,128]{1,0:T(8,128)S(1)}, u32[]{:S(2)}, u32[]{:S(2)}) collective-permute-start(f32[64,128]{1,0:T(8,128)} %get-tuple-element.32), channel_id=1, source_target_pairs={{32,0},{64,32},{96,64},{128,96},{160,128},{192,160},{224,192},{256... | collective-permute-start | bytes 98312 | tf_op jit(solution)/shard_map/ppermute | solution.py:498
  19.7 0.1 fusion.1
  20.0 0.1 pad_dynamic-slice_fusion.1
  20.1 0.2 copy.12
  20.3 0.1 reshape.12
  20.4 0.1 copy.11
  20.5 0.1 reshape.11
  20.6 0.7 div.14.k_ref.refs_0_
  21.3 0.6 concatenate.7.p_ref
  21.9 6.5 %matrices.1 = (bf16[192,192]{1,0:T(8,128)(2,1)}, bf16[192,240]{1,0:T(8,128)(2,1)}, bf16[4,256,256]{2,1,0:T(8,128)(2,1)}, bf16[4,256,256]{2,1,0:T(8,128)(2,1)}, b...) custom-call(f32[180]{0:T(256)} %div.14.k_ref.refs_0_), custom_call_target="tpu_custom_call" | custom-call | flops 8000000 | bytes 4000000 | tf_op jit(solution)/shard_map/matrices/pallas_call | solution.py:136
  28.5 0.6 copy-done.4
  29.0 0.6 copy-done.5
  29.6 1.9 %pack_rows.1 = (f32[216,256]{1,0:T(8,128)}, f32[216,256]{1,0:T(8,128)}) custom-call(f32[8,64,256]{2,1,0:T(8,128)} %e_ref.5, f32[64,128]{1,0:T(8,128)} %copy-done.4, f32[64,128]{1,0:T(8,128)} %copy-done.5), custom_call_target="tpu_custom_call" | custom-call | tf_op jit(solution)/shard_map/pack_rows/pallas_call | solution.py:206
  31.5 11.4 %collective-permute-start.2 = (f32[216,256]{1,0:T(8,128)}, f32[216,256]{1,0:T(8,128)S(1)}, u32[]{:S(2)}, u32[]{:S(2)}) collective-permute-start(f32[216,256]{1,0:T(8,128)} %get-tuple-element.33), channel_id=1, source_target_pairs={{0,1},{1,2},{2,3},{3,4},{4,5},{5,6},{6,7},{7,8},{8,9},{9,10},{10,1... | collective-permute-start | bytes 663560 | tf_op jit(solution)/shard_map/ppermute | solution.py:498
  42.9 1.9 %collective-permute-start.3 = (f32[216,256]{1,0:T(8,128)}, f32[216,256]{1,0:T(8,128)S(1)}, u32[]{:S(2)}, u32[]{:S(2)}) collective-permute-start(f32[216,256]{1,0:T(8,128)} %get-tuple-element.34), channel_id=1, source_target_pairs={{1,0},{2,1},{3,2},{4,3},{5,4},{6,5},{7,6},{8,7},{9,8},{10,9},{11,1... | collective-permute-start | bytes 663560 | tf_op jit(solution)/shard_map/ppermute | solution.py:498
  44.9 0.7 copy-done.10
  45.6 0.7 copy-done.11
  46.3 7.8 %warp.1 = (f32[4,8,48,256]{3,2,1,0:T(8,128)}, f32[4,8,48,128]{3,2,1,0:T(8,128)}, f32[4,8,48,256]{3,2,1,0:T(8,128)}, f32[4,8,48,128]{3,2,1,0:T(8,128)}) custom-call(s32[184]{0:T(256)} %concatenate.7.p_ref, f32[4,8,64,256]{3,2,1,0:T(8,128)} %v_ref.3, f32[4,64,256]{2,1,0:T(8,128)} %copy-done.10, f32[4,64,256]{2,1,0:T(8,128)} %copy-done.11), custom_call_target="tpu_custom_call" | custom-call | flops 6000000000 | bytes 8000000 | tf_op jit(solution)/shard_map/warp/pallas_call | solution.py:315
  54.1 12.0 %inner_rows.1.refs_18_ = f32[8,64,256]{2,1,0:T(8,128)} custom-call(f32[180]{0:T(256)} %div.14.k_ref.refs_0_, f32[8,64,256]{2,1,0:T(8,128)} %e_ref.5, f32[64,128]{1,0:T(8,128)} %copy-done.4, f32[64,128]{1,0:T(8,128)} %copy-done.5, f32[4,8,48,256]{3,2,1,0:T(8,128)} %get-tuple-element.49.refs_4_, f32[4,8,48,128]{3,2,1,0:T(8,128)} %get-tuple-element.50.refs_5_, ...), custom_call_target="tpu_custom_call" | custom-call | flops 6000000000 | bytes 12000000 | tf_op jit(solution)/shard_map/inner_rows/pallas_call | solution.py:455
  66.1 0.7 copy-done.12
  66.9 12.6 %edge_rows.1 = (f32[8,64,256]{2,1,0:T(8,128)}, f32[8,24,256]{2,1,0:T(8,128)}, f32[8,24,256]{2,1,0:T(8,128)}) custom-call(f32[180]{0:T(256)} %div.14.k_ref.refs_0_, f32[8,64,256]{2,1,0:T(8,128)} %e_ref.5, f32[64,128]{1,0:T(8,128)} %copy-done.4, f32[64,128]{1,0:T(8,128)} %copy-done.5, f32[216,256]{1,0:T(8,128)} %copy-done.12, f32[216,256]{1,0:T(8,128)} %copy-done.13, ...), custom_call_target="tpu_custom_call" | custom-call | flops 6000000000 | bytes 12000000 | tf_op jit(solution)/shard_map/edge_rows/pallas_call | solution.py:455
  79.5 7.5 %collective-permute-start.6 = (f32[8,24,256]{2,1,0:T(8,128)}, f32[8,24,256]{2,1,0:T(8,128)S(1)}, u32[]{:S(2)}, u32[]{:S(2)}) collective-permute-start(f32[8,24,256]{2,1,0:T(8,128)} %get-tuple-element.55), channel_id=1, source_target_pairs={{0,1},{1,2},{2,3},{3,4},{4,5},{5,6},{6,7},{7,8},{8,9},{9,10},{10,1... | collective-permute-start | bytes 589832 | tf_op jit(solution)/shard_map/ppermute | solution.py:498
  87.0 1.9 %collective-permute-start.7 = (f32[8,24,256]{2,1,0:T(8,128)}, f32[8,24,256]{2,1,0:T(8,128)S(1)}, u32[]{:S(2)}, u32[]{:S(2)}) collective-permute-start(f32[8,24,256]{2,1,0:T(8,128)} %get-tuple-element.56), channel_id=1, source_target_pairs={{1,0},{2,1},{3,2},{4,3},{5,4},{6,5},{7,6},{8,7},{9,8},{10,9},{11,1... | collective-permute-start | bytes 589832 | tf_op jit(solution)/shard_map/ppermute | solution.py:498
  89.0 3.1 %collective-permute-done.6.up_ref = f32[8,24,256]{2,1,0:T(8,128)S(1)} collective-permute-done((f32[8,24,256]{2,1,0:T(8,128)}, f32[8,24,256]{2,1,0:T(8,128)S(1)}, u32[]{:S(2)}, u32[]{:S(2)}) %collective-permute-start.6) | collective-permute-done | bytes 196640 | tf_op jit(solution)/shard_map/ppermute | solution.py:498
  92.1 8.2 %collective-permute-done.7.down_ref = f32[8,24,256]{2,1,0:T(8,128)S(1)} collective-permute-done((f32[8,24,256]{2,1,0:T(8,128)}, f32[8,24,256]{2,1,0:T(8,128)S(1)}, u32[]{:S(2)}, u32[]{:S(2)}) %collective-permute-start.7) | collective-permute-done | bytes 196640 | tf_op jit(solution)/shard_map/ppermute | solution.py:498
  100.3 0.7 copy-done.1
  101.0 2.2 %final.1 = f32[8,64,256]{2,1,0:T(8,128)} custom-call(f32[8,64,256]{2,1,0:T(8,128)} %e_ref.5, f32[8,64,256]{2,1,0:T(8,128)} %get-tuple-element.54.own_ref, f32[8,24,256]{2,1,0:T(8,128)} %copy-done, f32[8,24,256]{2,1,0:T(8,128)} %copy-done.1), custom_call_target="tpu_custom_call" | custom-call | tf_op jit(solution)/shard_map/final/pallas_call | solution.py:485
  (30 shorter events, 0.3 us)
Async XLA Ops:
  0.0 21.3 %copy-start.9 = (s32[2]{0:T(128)S(1)}, s32[2]{0:T(128)}, u32[]{:S(2)}) copy-start(s32[2]{0:T(128)} %constant.19.clone) | copy-start | bytes 28
  0.0 19.7 %copy-start.8 = (f32[4,15]{1,0:T(4,128)S(1)}, f32[4,15]{1,0:T(4,128)}, u32[]{:S(2)}) copy-start(f32[4,15]{1,0:T(4,128)} %param.10) | copy-start | bytes 724
  0.0 19.7 %copy-start.7 = (f32[4,15]{1,0:T(4,128)S(1)}, f32[4,15]{1,0:T(4,128)}, u32[]{:S(2)}) copy-start(f32[4,15]{1,0:T(4,128)} %param.11) | copy-start | bytes 724
  0.0 19.7 %copy-start.6 = (f32[4,15]{1,0:T(4,128)S(1)}, f32[4,15]{1,0:T(4,128)}, u32[]{:S(2)}) copy-start(f32[4,15]{1,0:T(4,128)} %param.12) | copy-start | bytes 724
  0.0 19.9 %copy-start.2 = (s32[4,3,32,16]{2,3,1,0:T(8,128)S(1)}, s32[4,3,32,16]{2,3,1,0:T(8,128)}, u32[]{:S(2)}) copy-start(s32[4,3,32,16]{2,3,1,0:T(8,128)} %param.14) | copy-start | bytes 73732
  0.0 20.0 %copy-start.3 = (s32[4,2,32,16]{2,3,1,0:T(8,128)S(1)}, s32[4,2,32,16]{2,3,1,0:T(8,128)}, u32[]{:S(2)}) copy-start(s32[4,2,32,16]{2,3,1,0:T(8,128)} %param.13) | copy-start | bytes 49156
  3.0 41.8 %collective-permute-start.4 = (f32[4,64,256]{2,1,0:T(8,128)}, f32[4,64,256]{2,1,0:T(8,128)S(1)}, u32[]{:S(2)}, u32[]{:S(2)}) collective-permute-start(f32[4,64,256]{2,1,0:T(8,128)} %get-tuple-element.35), channel_id=1, source_target_pairs={{0,32},{32,64},{64,96},{96,128},{128,160},{160,192},{192,224},{224... | collective-permute-start | bytes 786440 | tf_op jit(solution)/shard_map/ppermute | solution.py:498
  6.2 38.7 %collective-permute-start.5 = (f32[4,64,256]{2,1,0:T(8,128)}, f32[4,64,256]{2,1,0:T(8,128)S(1)}, u32[]{:S(2)}, u32[]{:S(2)}) collective-permute-start(f32[4,64,256]{2,1,0:T(8,128)} %get-tuple-element.36), channel_id=1, source_target_pairs={{32,0},{64,32},{96,64},{128,96},{160,128},{192,160},{224,192},{256... | collective-permute-start | bytes 786440 | tf_op jit(solution)/shard_map/ppermute | solution.py:498
  12.3 16.2 %collective-permute-start = (f32[64,128]{1,0:T(8,128)}, f32[64,128]{1,0:T(8,128)S(1)}, u32[]{:S(2)}, u32[]{:S(2)}) collective-permute-start(f32[64,128]{1,0:T(8,128)} %get-tuple-element.31), channel_id=1, source_target_pairs={{0,32},{32,64},{64,96},{96,128},{128,160},{160,192},{192,224},{224... | collective-permute-start | bytes 98312 | tf_op jit(solution)/shard_map/ppermute | solution.py:498
  14.2 14.3 %collective-permute-start.1 = (f32[64,128]{1,0:T(8,128)}, f32[64,128]{1,0:T(8,128)S(1)}, u32[]{:S(2)}, u32[]{:S(2)}) collective-permute-start(f32[64,128]{1,0:T(8,128)} %get-tuple-element.32), channel_id=1, source_target_pairs={{32,0},{64,32},{96,64},{128,96},{160,128},{192,160},{224,192},{256... | collective-permute-start | bytes 98312 | tf_op jit(solution)/shard_map/ppermute | solution.py:498
  28.4 0.6 copy-start.4
  29.0 0.6 copy-start.5
  31.5 34.6 %collective-permute-start.2 = (f32[216,256]{1,0:T(8,128)}, f32[216,256]{1,0:T(8,128)S(1)}, u32[]{:S(2)}, u32[]{:S(2)}) collective-permute-start(f32[216,256]{1,0:T(8,128)} %get-tuple-element.33), channel_id=1, source_target_pairs={{0,1},{1,2},{2,3},{3,4},{4,5},{5,6},{6,7},{7,8},{8,9},{9,10},{10,1... | collective-permute-start | bytes 663560 | tf_op jit(solution)/shard_map/ppermute | solution.py:498
  42.9 23.2 %collective-permute-start.3 = (f32[216,256]{1,0:T(8,128)}, f32[216,256]{1,0:T(8,128)S(1)}, u32[]{:S(2)}, u32[]{:S(2)}) collective-permute-start(f32[216,256]{1,0:T(8,128)} %get-tuple-element.34), channel_id=1, source_target_pairs={{1,0},{2,1},{3,2},{4,3},{5,4},{6,5},{7,6},{8,7},{9,8},{10,9},{11,1... | collective-permute-start | bytes 663560 | tf_op jit(solution)/shard_map/ppermute | solution.py:498
  44.9 0.7 copy-start.10
  45.6 0.7 copy-start.11
  66.1 0.7 copy-start.12
  66.1 0.8 copy-start.13
  79.5 12.6 %collective-permute-start.6 = (f32[8,24,256]{2,1,0:T(8,128)}, f32[8,24,256]{2,1,0:T(8,128)S(1)}, u32[]{:S(2)}, u32[]{:S(2)}) collective-permute-start(f32[8,24,256]{2,1,0:T(8,128)} %get-tuple-element.55), channel_id=1, source_target_pairs={{0,1},{1,2},{2,3},{3,4},{4,5},{5,6},{6,7},{7,8},{8,9},{9,10},{10,1... | collective-permute-start | bytes 589832 | tf_op jit(solution)/shard_map/ppermute | solution.py:498
  87.0 13.3 %collective-permute-start.7 = (f32[8,24,256]{2,1,0:T(8,128)}, f32[8,24,256]{2,1,0:T(8,128)S(1)}, u32[]{:S(2)}, u32[]{:S(2)}) collective-permute-start(f32[8,24,256]{2,1,0:T(8,128)} %get-tuple-element.56), channel_id=1, source_target_pairs={{1,0},{2,1},{3,2},{4,3},{5,4},{6,5},{7,6},{8,7},{9,8},{10,9},{11,1... | collective-permute-start | bytes 589832 | tf_op jit(solution)/shard_map/ppermute | solution.py:498
  92.1 8.2 %copy-start = (f32[8,24,256]{2,1,0:T(8,128)}, f32[8,24,256]{2,1,0:T(8,128)S(1)}, u32[]{:S(2)}) copy-start(f32[8,24,256]{2,1,0:T(8,128)S(1)} %collective-permute-done.6.up_ref) | copy-start | bytes 589828
  100.3 0.7 copy-start.1
where the time goes:
time: 104 us; the launch traced here: 103 us
  Pallas kernels  47.8 us (46%)
  starting transfers between devices  37.5 us (36%)
  waiting for transfers between devices  11.4 us (11%)
  local copies, waits for them, and re-layouts  6.03 us (6%)
    ppermute x8, starting transfers between devices, shifted(): return (lax.ppermute(last, axis, up), lax.ppermute(first, axis, down))  37.5 us
    pallas_call x2, Pallas kernels, main(): pl.pallas_call(functools.partial(main_kernel, inner), out_shape=[own] if...  24.6 us
    ppermute x8, waiting for transfers between devices, shifted(): return (lax.ppermute(last, axis, up), lax.ppermute(first, axis, down))  11.4 us
    pallas_call x1, Pallas kernels, warp(): pl.pallas_call(warp_kernel, grid=(VIEWS,), out_shape=[w, s, w, s], in_spe...  7.78 us
    pallas_call x1, Pallas kernels, matrices(): pl.pallas_call(matrices_kernel, out_shape=[jax.ShapeDtypeStruct(s, BF16)...  6.51 us
    unnamed x28, local copies, waits for them, and re-layouts  4.04 us
    pallas_call x1, Pallas kernels, pack_views(): pl.pallas_call(pack_views_kernel, out_shape=[jax.ShapeDtypeStruct((VIEWS,...  3 us
    pallas_call x1, Pallas kernels, final(): pl.pallas_call(final_kernel, out_shape=jax.ShapeDtypeStruct((Z, ROWS, COL...  2.17 us
  transfers between devices with their start and end apart: 8, of which 2 were waited for; matrix products, arithmetic and copies ran while one was open for 2% of the time, Pallas kernels for 29%

commit v1 on v0

--- a/solution.py
+++ b/solution.py
@@ -19,6 +19,13 @@
 
 SMEM = pl.BlockSpec(memory_space=pltpu.SMEM)
 VMEM = pl.BlockSpec(memory_space=pltpu.VMEM)
+
+
+EDGES = pl.BlockSpec((ROWS, COLS), lambda *g: (VIEWS, 0))
+
+
+def limit(mib):
+    return pltpu.CompilerParams(vmem_limit_bytes=mib << 20)
 
 
 def iota(shape, dim):
@@ -78,51 +85,64 @@
             high = weight.astype(BF16).astype(F32)
             ly[v * SET : (v + 1) * SET, :] = jnp.where(seg < 2, high, weight - high).astype(BF16)
 
+    view = iota((1, VIEWS * SET), 1) // SET
+    taps = []
+    for tap in range(TAPS):
+        value = jnp.full(view.shape, k_ref[ky + tap])
+        for v in range(1, VIEWS):
+            value = jnp.where(view == v, k_ref[ky + v * TAPS + tap], value)
+        taps.append(value)
     for inner, m_ref, n_ref in ((True, m_i, n_i), (False, m_o, n_o)):
         shape = (output_rows(inner), VIEWS * SET)
         lane = iota(shape, 1)
-        view = lane // SET
-        differ = output_row(inner, iota(shape, 0)) - sample_row(inner, lane - view * SET) + 7
+        differ = output_row(inner, iota(shape, 0)) - sample_row(inner, lane - (lane // SET) * SET) + 7
         weight = jnp.zeros(shape, F32)
-        for v in range(VIEWS):
-            weight = jnp.where(view == v, band(k_ref, ky + v * TAPS, differ), weight)
+        for tap in range(TAPS):
+            weight = jnp.where(differ == tap, taps[tap], weight)
         high, low = split(weight)
         m_ref[...] = high
         n_ref[...] = low
 
     def per_view(v, carry):
         base = kx + v * TAPS
-        differ = iota((COLS, COLS), 0) - iota((COLS, COLS), 1) + 7
-        high, low = split(band(k_ref, base, differ))
-        f_hi[v] = high
-        f_lo[v] = low
-        high, low = split(band(k_ref, base, 14 - differ))
-        b_hi[v] = high
-        b_lo[v] = low
+        differ = iota((128, 128), 0) - iota((128, 128), 1) + 7
+        corner = iota((16, 128), 0) - iota((16, 128), 1)
+        for mirrored, hi_ref, lo_ref in ((False, f_hi, f_lo), (True, b_hi, b_lo)):
+            def parts(d):
+                return split(band(k_ref, base, 14 - d if mirrored else d))
+
+            diagonal, lower, upper = parts(differ), parts(corner + 135), parts(corner - 9)
+            for ref, a, b, c in zip((hi_ref, lo_ref), diagonal, lower, upper):
+                ref[v, 0:128, 0:128] = a
+                ref[v, 128:256, 128:256] = a
+                ref[v, 128:144, 0:128] = b
+                ref[v, 144:256, 0:128] = jnp.zeros((112, 128), BF16)
+                ref[v, 112:128, 128:256] = c
+                ref[v, 0:112, 128:256] = jnp.zeros((112, 128), BF16)
         for out_ref, width in ((f_t, COLS), (f_s, 128)):
-            shape = (256, width)
-            row = iota(shape, 0)
-            second = row >= 128
-            h = jnp.where(second, row - 128, row)
-            place = jnp.where(h < 48, h, h - 48)
+            shape = (48, width)
+            place = iota(shape, 0)
             source = jnp.where(
                 place < 16,
                 place - 16,
                 jnp.where(place < 32, place + 240, jnp.where(place < 40, place - 32, place + 208)),
             )
-            limit = 32 if width == COLS else 48
-            good = (place < limit) & (h < jnp.where(second, 48, 96))
             target = iota(shape, 1) if width == COLS else strip_col(iota(shape, 1))
-            weight = band(k_ref, base, jnp.where(good, source - target + 7, -1))
-            high = weight.astype(BF16).astype(F32)
-            out_ref[v] = jnp.where(second, weight - high, high).astype(BF16)
-        shape = (128, COLS)
-        row = iota(shape, 0)
-        seg = row // 16
-        differ = iota(shape, 1) - strip_col(row - seg * 16) + 7
-        weight = band(k_ref, base, jnp.where(seg < 3, differ, -1))
-        high = weight.astype(BF16).astype(F32)
-        b_t[v] = jnp.where(seg < 2, high, weight - high).astype(BF16)
+            differ = source - target + 7
+            if width == COLS:
+                differ = jnp.where(place < 32, differ, -1)
+            high, low = split(band(k_ref, base, differ))
+            out_ref[v, 0:48] = high
+            out_ref[v, 48:96] = high
+            out_ref[v, 96:128] = jnp.zeros((32, width), BF16)
+            out_ref[v, 128:176] = low
+            out_ref[v, 176:256] = jnp.zeros((80, width), BF16)
+        shape = (16, COLS)
+        high, low = split(band(k_ref, base, iota(shape, 1) - strip_col(iota(shape, 0)) + 7))
+        b_t[v, 0:16] = high
+        b_t[v, 16:32] = high
+        b_t[v, 32:48] = low
+        b_t[v, 48:128] = jnp.zeros((80, COLS), BF16)
         return carry
 
     lax.fori_loop(0, VIEWS, per_view, 0)
@@ -139,77 +159,82 @@
         in_specs=[SMEM],
         out_specs=[VMEM] * len(shapes),
         name="matrices",
+        compiler_params=limit(12),
         cost_estimate=pl.CostEstimate(flops=8_000_000, bytes_accessed=4_000_000, transcendentals=0),
     )(kernels)
 
 
-def pack_estimate_kernel(e_ref, left_ref, right_ref):
-    lane = iota((ROWS, 128), 1) // 16
-    left = jnp.zeros((ROWS, 128), F32)
-    right = jnp.zeros((ROWS, 128), F32)
-    for z in range(Z):
-        a = pltpu.roll(e_ref[z, :, 0:128], z * 16, 1) if z else e_ref[z, :, 0:128]
-        b = pltpu.roll(e_ref[z, :, 128:256], (z * 16 + 16) % 128, 1) if z < 7 else e_ref[z, :, 128:256]
-        left = jnp.where(lane == z, a, left)
-        right = jnp.where(lane == z, b, right)
-    left_ref[...] = left
-    right_ref[...] = right
-
-
-def pack_estimate(estimate):
+def pack_edges_kernel(e_ref, v_ref, left_ref, right_ref):
+    def fill(ref, count, width, base, lanes):
+        lane = iota((ROWS, 128), 1) // width
+        left = jnp.zeros((ROWS, 128), F32)
+        right = jnp.zeros((ROWS, 128), F32)
+        for q in range(count):
+            a, b = ref(base + q, slice(0, 128)), ref(base + q, slice(128, 256))
+            turn = (q * width + width) % 128
+            a = pltpu.roll(a, q * width, 1) if q else a
+            b = pltpu.roll(b, turn, 1) if turn else b
+            left = jnp.where(lane == q, a, left)
+            right = jnp.where(lane == q, b, right)
+        left_ref[:, lanes] = left
+        right_ref[:, lanes] = right
+
+    @pl.when(pl.program_id(0) < VIEWS)
+    def _():
+        for half in range(2):
+            fill(lambda z, cols: v_ref[0, z, :, cols], 4, 24, half * 4, slice(half * 128, half * 128 + 128))
+
+    @pl.when(pl.program_id(0) == VIEWS)
+    def _():
+        fill(lambda z, cols: e_ref[z, :, cols], Z, 16, 0, slice(0, 128))
+        for ref in (left_ref, right_ref):
+            ref[:, 128:256] = jnp.zeros((ROWS, 128), F32)
+
+
+def pack_edges(estimate, views):
+    out = jax.ShapeDtypeStruct(((VIEWS + 1) * ROWS, COLS), F32)
+    spec = pl.BlockSpec((ROWS, COLS), lambda g: (g, 0))
     return pl.pallas_call(
-        pack_estimate_kernel,
-        out_shape=[jax.ShapeDtypeStruct((ROWS, 128), F32)] * 2,
-        in_specs=[VMEM],
-        out_specs=[VMEM] * 2,
-        name="pack_estimate",
-    )(estimate)
-
-
-def pack_views_kernel(v_ref, left_ref, right_ref):
-    lane = iota((ROWS, 128), 1) // 24
-    for v in range(VIEWS):
-        for half in range(2):
-            left = jnp.zeros((ROWS, 128), F32)
-            right = jnp.zeros((ROWS, 128), F32)
-            for q in range(4):
-                z = half * 4 + q
-                a = v_ref[v, z, :, 0:128]
-                a = pltpu.roll(a, q * 24, 1) if q else a
-                b = pltpu.roll(v_ref[v, z, :, 128:256], q * 24 + 24, 1)
-                left = jnp.where(lane == q, a, left)
-                right = jnp.where(lane == q, b, right)
-            left_ref[v, :, half * 128 : half * 128 + 128] = left
-            right_ref[v, :, half * 128 : half * 128 + 128] = right
-
-
-def pack_views(views):
-    return pl.pallas_call(
-        pack_views_kernel,
-        out_shape=[jax.ShapeDtypeStruct((VIEWS, ROWS, COLS), F32)] * 2,
-        in_specs=[VMEM],
-        out_specs=[VMEM] * 2,
-        name="pack_views",
-        cost_estimate=pl.CostEstimate(flops=1_000_000, bytes_accessed=2_600_000, transcendentals=0),
-    )(views)
+        pack_edges_kernel,
+        grid=(VIEWS + 1,),
+        out_shape=[out, out],
+        in_specs=[
+            pl.BlockSpec((Z, ROWS, COLS), lambda g: (0, 0, 0)),
+            pl.BlockSpec((1, Z, ROWS, COLS), lambda g: (jnp.minimum(g, VIEWS - 1), 0, 0, 0)),
+        ],
+        out_specs=[spec, spec],
+        name="pack_edges",
+        compiler_params=limit(12),
+        cost_estimate=pl.CostEstimate(flops=1_000_000, bytes_accessed=3_200_000, transcendentals=0),
+    )(estimate, views)
 
 
 def pack_rows_kernel(e_ref, l_ref, r_ref, first_ref, last_ref):
     for out_ref, start in ((first_ref, 0), (last_ref, ROWS - EDGE)):
         for z in range(Z):
             out_ref[z * EDGE : (z + 1) * EDGE, :] = e_ref[z, start : start + EDGE, :]
-        out_ref[Z * EDGE :, 0:128] = l_ref[start : start + EDGE, :]
-        out_ref[Z * EDGE :, 128:256] = r_ref[start : start + EDGE, :]
+        out_ref[Z * EDGE :, 0:128] = l_ref[start : start + EDGE, 0:128]
+        out_ref[Z * EDGE :, 128:256] = r_ref[start : start + EDGE, 0:128]
 
 
 def pack_rows(estimate, left, right):
     return pl.pallas_call(
         pack_rows_kernel,
         out_shape=[jax.ShapeDtypeStruct(((Z + 1) * EDGE, COLS), F32)] * 2,
-        in_specs=[VMEM] * 3,
+        in_specs=[VMEM, EDGES, EDGES],
         out_specs=[VMEM] * 2,
+        grid=(1,),
         name="pack_rows",
+        compiler_params=limit(12),
     )(estimate, left, right)
+
+
+def planes_to_lanes(parts):
+    lane = iota(parts[0].shape, 1) // 16
+    total = parts[0]
+    for z in range(1, Z):
+        total = jnp.where(lane == z, pltpu.roll(parts[z], 16 * z, 1), total)
+    return total
 
 
 def warp_kernel(p_ref, v_ref, l_ref, r_ref, wi_ref, si_ref, wo_ref, so_ref,
@@ -220,8 +245,8 @@
     for z in range(Z):
         q, half = z % 4, z // 4
         a, b = v_ref[0, z, :, 0:128], v_ref[0, z, :, 128:256]
-        left = l_ref[0, :, half * 128 : half * 128 + 128]
-        right = r_ref[0, :, half * 128 : half * 128 + 128]
+        left = l_ref[:, half * 128 : half * 128 + 128]
+        right = r_ref[:, half * 128 : half * 128 + 128]
         left = pltpu.roll(left, (128 - q * 24) % 128, 1) if q else left
         right = pltpu.roll(right, (128 + 24 - q * 24) % 128, 1) if q != 1 else right
         edge = jnp.where(lane < 24, left, jnp.where(lane < 48, right, jnp.where(
@@ -296,22 +321,26 @@
         w += jnp.dot(c_lo[rows], x_map, preferred_element_type=F32)
         s = jnp.dot(s_hi[rows], s_map, preferred_element_type=F32)
         s += jnp.dot(s_lo[rows], s_map, preferred_element_type=F32)
-        for value, i_ref, o_ref in ((w, wi_ref, wo_ref), (s, si_ref, so_ref)):
-            for z in range(Z):
-                if b == 1:
-                    i_ref[0, z] = value[z * 64 : z * 64 + 48]
-                    o_ref[0, z, 0:16] = value[z * 64 + 48 : z * 64 + 64]
-                else:
-                    at = 16 if b == 0 else 32
-                    o_ref[0, z, at : at + 16] = value[z * 16 : z * 16 + 16]
+        at = 0 if b == 1 else (16 if b == 0 else 32)
+        for z in range(Z):
+            if b == 1:
+                wi_ref[0, z] = w[z * 64 : z * 64 + 48]
+                wo_ref[0, z, 0:16] = w[z * 64 + 48 : z * 64 + 64]
+            else:
+                wo_ref[0, z, at : at + 16] = w[z * 16 : z * 16 + 16]
+        if b == 1:
+            si_ref[0] = planes_to_lanes([s[z * 64 : z * 64 + 48] for z in range(Z)])
+            so_ref[0, 0:16] = planes_to_lanes([s[z * 64 + 48 : z * 64 + 64] for z in range(Z)])
+        else:
+            so_ref[0, at : at + 16] = planes_to_lanes([s[z * 16 : z * 16 + 16] for z in range(Z)])
 
 
 def warp(params, views, left, right):
     w = jax.ShapeDtypeStruct((VIEWS, Z, SET, COLS), F32)
-    s = jax.ShapeDtypeStruct((VIEWS, Z, SET, 128), F32)
+    s = jax.ShapeDtypeStruct((VIEWS, SET, 128), F32)
     w_spec = pl.BlockSpec((1, Z, SET, COLS), lambda v: (v, 0, 0, 0))
-    s_spec = pl.BlockSpec((1, Z, SET, 128), lambda v: (v, 0, 0, 0))
-    side = pl.BlockSpec((1, ROWS, COLS), lambda v: (v, 0, 0))
+    s_spec = pl.BlockSpec((1, SET, 128), lambda v: (v, 0, 0))
+    side = pl.BlockSpec((ROWS, COLS), lambda v: (v, 0))
     return pl.pallas_call(
         warp_kernel,
         grid=(VIEWS,),
@@ -326,6 +355,7 @@
             pltpu.VMEM((768, 256), BF16),
         ],
         name="warp",
+        compiler_params=limit(20),
         cost_estimate=pl.CostEstimate(flops=6_000_000_000, bytes_accessed=8_000_000, transcendentals=0),
     )(params, views, left, right)
 
@@ -343,14 +373,14 @@
         out_refs, refs = refs[:1], refs[1:]
     else:
         partial_ref, out_refs, refs = refs[0], refs[1:4], refs[4:]
-    d, g_hi, g_lo, g_t, cen, stp, q_hi, q_lo, q_t, x2 = refs
+    d, g_hi, g_lo, g_t, cen, q_hi, q_lo, q_t, x2 = refs
     count = estimate_rows(inner)
     lane = iota((count, 128), 1)
     lane_out = iota((VIEWS * SET, 128), 1)
     for z in range(Z):
         if inner:
             c0, c1 = e_ref[z, :, 0:128], e_ref[z, :, 128:256]
-            lh, rh = l_ref[...], r_ref[...]
+            lh, rh = l_ref[:, 0:128], r_ref[:, 0:128]
         else:
             edge = slice(z * EDGE, (z + 1) * EDGE)
             tail = slice(Z * EDGE, (Z + 1) * EDGE)
@@ -362,9 +392,9 @@
             c0 = rows(slice(0, 128), e_ref[z, :, 0:128])
             c1 = rows(slice(128, 256), e_ref[z, :, 128:256])
             lh = jnp.concatenate(
-                [above[tail, 0:128], l_ref[0:16], l_ref[48:64], below[tail, 0:128]], axis=0)
+                [above[tail, 0:128], l_ref[0:16, 0:128], l_ref[48:64, 0:128], below[tail, 0:128]], axis=0)
             rh = jnp.concatenate(
-                [above[tail, 128:256], r_ref[0:16], r_ref[48:64], below[tail, 128:256]], axis=0)
+                [above[tail, 128:256], r_ref[0:16, 0:128], r_ref[48:64, 0:128], below[tail, 128:256]], axis=0)
         lh = pltpu.roll(lh, (128 - z * 16) % 128, 1) if z else lh
         rh = pltpu.roll(rh, (128 + 16 - z * 16) % 128, 1) if z != 1 else rh
         h = jnp.where(lane < 16, lh, jnp.where(lane < 32, rh, jnp.where(
@@ -388,52 +418,59 @@
             g_t[v, to, 0:128] = both[at]
             g_t[v, to, 128:256] = high[at, 256:384]
 
-    def per_view(v, carry):
-        def dot(a, b):
-            return jnp.dot(a, b, preferred_element_type=F32)
-
-        cen[...] = (dot(g_hi[v], f_hi[v]) + dot(g_lo[v], f_hi[v])) + (
+    def dot(a, b):
+        return jnp.dot(a, b, preferred_element_type=F32)
+
+    plane = iota((SET, 128), 1) // 16
+    lanes = iota((SET, 128), 1)
+
+    def turn(value, by):
+        return pltpu.roll(value, by % 128, 1) if by % 128 else value
+
+    for v in range(VIEWS):
+        cen[v] = (dot(g_hi[v], f_hi[v]) + dot(g_lo[v], f_hi[v])) + (
             dot(g_hi[v], f_lo[v]) + dot(g_t[v], f_t[v]))
-        stp[...] = dot(g_t[v], f_s[v])
+        strip = dot(g_t[v], f_s[v])
         taps = [k_ref[2 * VIEWS * TAPS + v * TAPS + t] for t in range(TAPS)]
         for rb in range(3):
-            for t in range(3):
-                ref, cols = (cen, slice(t * 128, t * 128 + 128)) if t < 2 else (stp, slice(0, 128))
+            for t in range(2):
+                cols = slice(t * 128, t * 128 + 128)
                 at = [slice(z * SET + rb * 16, z * SET + rb * 16 + 16) for z in range(Z)]
-                f = [ref[at[z], cols] for z in range(Z)]
+                f = [cen[v, at[z], cols] for z in range(Z)]
                 ratio = []
                 for z in range(Z):
                     total = taps[7 - z] * f[0]
                     for y in range(1, Z):
                         total = total + taps[y - z + 7] * f[y]
                     total = jnp.where(total == 0.0, 1.0, total)
-                    rows = slice(rb * 16, rb * 16 + 16)
-                    top = w_ref[v, z, rows, cols] if t < 2 else s_ref[v, z, rows, cols]
-                    ratio.append(top / total)
+                    ratio.append(w_ref[v, z, rb * 16 : rb * 16 + 16, cols] / total)
                 for z in range(Z):
                     total = taps[z + 7] * ratio[0]
                     for y in range(1, Z):
                         total = total + taps[z - y + 7] * ratio[y]
-                    if t < 2:
-                        high, low = split(total)
-                        q_hi[at[z], cols] = high
-                        q_lo[at[z], cols] = low
-                    else:
-                        high = total.astype(BF16).astype(F32)
-                        low = total - high
-                        lanes = iota((16, 128), 1)
-                        q_t[at[z], :] = jnp.where(lanes < 16, high, jnp.where(
-                            lanes < 32, pltpu.roll(low, 16, 1), jnp.where(
-                                lanes < 48, pltpu.roll(high, 32, 1), 0.0))).astype(BF16)
-        x = (dot(q_hi[...], b_hi[v]) + dot(q_lo[...], b_hi[v])) + (
-            dot(q_hi[...], b_lo[v]) + dot(q_t[...], b_t[v]))
+                    high, low = split(total)
+                    q_hi[v, at[z], cols] = high
+                    q_lo[v, at[z], cols] = low
+        strip = planes_to_lanes([strip[z * SET : (z + 1) * SET] for z in range(Z)])
+        total = taps[7] * strip
+        for y in range(1, Z):
+            total = total + jnp.where(plane < Z - y, taps[7 + y], taps[y - 1]) * turn(strip, -16 * y)
+        ratio = s_ref[v] / jnp.where(total == 0.0, 1.0, total)
+        total = taps[7] * ratio
+        for y in range(1, Z):
+            total = total + jnp.where(plane < Z - y, taps[7 - y], taps[15 - y]) * turn(ratio, -16 * y)
+        high = total.astype(BF16).astype(F32)
+        low = total - high
+        for z in range(Z):
+            q_t[v, z * SET : (z + 1) * SET, :] = jnp.where(lanes < 16, turn(high, -16 * z), jnp.where(
+                lanes < 32, turn(low, 16 - 16 * z), jnp.where(
+                    lanes < 48, turn(high, 32 - 16 * z), 0.0))).astype(BF16)
+        x = (dot(q_hi[v], b_hi[v]) + dot(q_lo[v], b_hi[v])) + (
+            dot(q_hi[v], b_lo[v]) + dot(q_t[v], b_t[v]))
         high, low = split(x)
         for z in range(Z):
             x2[z, 0, v] = high[z * SET : (z + 1) * SET]
             x2[z, 1, v] = low[z * SET : (z + 1) * SET]
-        return carry
-
-    lax.fori_loop(0, VIEWS, per_view, 0)
     for z in range(Z):
         high = x2[z, 0].reshape(VIEWS * SET, COLS)
         low = x2[z, 1].reshape(VIEWS * SET, COLS)
@@ -455,39 +492,23 @@
     return pl.pallas_call(
         functools.partial(main_kernel, inner),
         out_shape=[own] if inner else [own, edge, edge],
-        in_specs=[SMEM] + [VMEM] * (len(args) - 1),
+        grid=(1,),
+        in_specs=[SMEM, VMEM, EDGES, EDGES] + [VMEM] * (len(args) - 4),
         out_specs=[VMEM] * (1 if inner else 3),
         scratch_shapes=[
             pltpu.VMEM((3 * estimate_rows(inner), 384), BF16),
             pltpu.VMEM((VIEWS, rows, 256), BF16),
             pltpu.VMEM((VIEWS, rows, 256), BF16),
             pltpu.VMEM((VIEWS, rows, 256), BF16),
-            pltpu.VMEM((rows, 256), F32),
-            pltpu.VMEM((rows, 128), F32),
-            pltpu.VMEM((rows, 256), BF16),
-            pltpu.VMEM((rows, 256), BF16),
-            pltpu.VMEM((rows, 128), BF16),
+            pltpu.VMEM((VIEWS, rows, 256), F32),
+            pltpu.VMEM((VIEWS, rows, 256), BF16),
+            pltpu.VMEM((VIEWS, rows, 256), BF16),
+            pltpu.VMEM((VIEWS, rows, 128), BF16),
             pltpu.VMEM((Z, 2, VIEWS, SET, COLS), BF16),
         ],
         name="inner_rows" if inner else "edge_rows",
+        compiler_params=limit(28),
         cost_estimate=pl.CostEstimate(flops=6_000_000_000, bytes_accessed=12_000_000, transcendentals=0),
-    )(*args)
-
-
-def final_kernel(e_ref, own_ref, up_ref, down_ref, out_ref):
-    for z in range(Z):
-        out_ref[z, 0:24] = e_ref[z, 0:24] * ((own_ref[z, 0:24] + up_ref[z]) * 0.25)
-        out_ref[z, 24:40] = e_ref[z, 24:40] * (own_ref[z, 24:40] * 0.25)
-        out_ref[z, 40:64] = e_ref[z, 40:64] * ((own_ref[z, 40:64] + down_ref[z]) * 0.25)
-
-
-def final(*args):
-    return pl.pallas_call(
-        final_kernel,
-        out_shape=jax.ShapeDtypeStruct((Z, ROWS, COLS), F32),
-        in_specs=[VMEM] * 4,
-        out_specs=VMEM,
-        name="final",
     )(*args)
 
 
@@ -511,18 +532,20 @@
     params = jnp.concatenate(
         [neighbours(block_offsets, j, i), neighbours(sub_shifts, j, i), j[None], i[None],
          jnp.array([lax.axis_size("gy") - 1, lax.axis_size("gx") - 1], jnp.int32)])
-    e_left, e_right = shifted(*pack_estimate(estimate), "gx")
+    left, right = shifted(*pack_edges(estimate, views), "gx")
     mats = matrices(kernels)
     ly_i, ly_o, *x_mats, m_i, n_i, m_o, n_o = mats
-    above, below = shifted(*pack_rows(estimate, e_left, e_right), "gy")
-    v_left, v_right = shifted(*pack_views(views), "gx")
-    w_i, s_i, w_o, s_o = warp(params, views, v_left, v_right)
-    (inside,) = main(True, kernels, estimate, e_left, e_right, w_i, s_i, ly_i, *x_mats, m_i, n_i)
+    above, below = shifted(*pack_rows(estimate, left, right), "gy")
+    w_i, s_i, w_o, s_o = warp(params, views, left, right)
+    (inside,) = main(True, kernels, estimate, left, right, w_i, s_i, ly_i, *x_mats, m_i, n_i)
     own, up, down = main(
-        False, kernels, estimate, e_left, e_right, above, below, w_o, s_o, ly_o, *x_mats,
+        False, kernels, estimate, left, right, above, below, w_o, s_o, ly_o, *x_mats,
         m_o, n_o, inside)
     from_above, from_below = shifted(up, down, "gy")
-    return final(estimate, own, from_above, from_below)
+    rest = ROWS - EDGE
+    total = own + jnp.pad(from_above, ((0, 0), (0, rest), (0, 0)))
+    total = total + jnp.pad(from_below, ((0, 0), (rest, 0), (0, 0)))
+    return estimate * (total * 0.25)
 
 
 def solution(mesh):

time: 104 us -> 78.5 us (0.75)
  the two profiles are of different devices: /device:TPU:89 before, /device:TPU:39 now
where the time goes in v1:
time: 78.5 us; the launch traced here: 78.1 us
  starting transfers between devices  28.7 us (37%)
  Pallas kernels  24.9 us (32%)
  waiting for transfers between devices  18.8 us (24%)
  local copies, waits for them, and re-layouts  4.45 us (6%)
  other arithmetic  1.09 us (1%)
    ppermute x6, starting transfers between devices, shifted(): return (lax.ppermute(last, axis, up), lax.ppermute(first, axis, down))  28.7 us
    ppermute x6, waiting for transfers between devices, shifted(): return (lax.ppermute(last, axis, up), lax.ppermute(first, axis, down))  18.8 us
    pallas_call x2, Pallas kernels, main(): pl.pallas_call(functools.partial(main_kernel, inner), out_shape=[own] if...  13.5 us
    pallas_call x1, Pallas kernels, warp(): pl.pallas_call(warp_kernel, grid=(VIEWS,), out_shape=[w, s, w, s], in_spe...  6.44 us
    unnamed x18, local copies, waits for them, and re-layouts  2.66 us
    pallas_call x1, Pallas kernels, pack_edges(): pl.pallas_call(pack_edges_kernel, grid=(VIEWS + 1,), out_shape=[out, out]...  2.52 us
    pallas_call x1, Pallas kernels, matrices(): pl.pallas_call(matrices_kernel, out_shape=[jax.ShapeDtypeStruct(s, BF16)...  2.39 us
  transfers between devices with their start and end apart: 6, of which 4 were waited for; matrix products, arithmetic and copies ran while one was open for 3% of the time, Pallas kernels for 20%

profile of v1, /device:TPU:39, one launch (start us, length us, event | category | flops | bytes accessed | tf_op | source)
XLA Modules:
  0.0 78.1 jit_solution(14453520622046781132)
XLA Ops:
  0.0 1.0 %copy-done = f32[8,64,256]{2,1,0:T(8,128)S(1)} copy-done((f32[8,64,256]{2,1,0:T(8,128)S(1)}, f32[8,64,256]{2,1,0:T(8,128)}, u32[]{:S(2)}) %copy-start) | copy-done | bytes 524312
  1.0 1.6 %copy-done.2 = f32[4,8,64,256]{3,2,1,0:T(8,128)S(1)} copy-done((f32[4,8,64,256]{3,2,1,0:T(8,128)S(1)}, f32[4,8,64,256]{3,2,1,0:T(8,128)}, u32[]{:S(2)}) %copy-start.2) | copy-done | bytes 2097176
  2.6 0.0 copy-start.8
  2.7 2.5 %pack_edges.1 = (f32[320,256]{1,0:T(8,128)}, f32[320,256]{1,0:T(8,128)}) custom-call(f32[8,64,256]{2,1,0:T(8,128)S(1)} %copy-done, f32[4,8,64,256]{3,2,1,0:T(8,128)S(1)} %copy-done.2), custom_call_target="tpu_custom_call" | custom-call | flops 1000000 | bytes 3200000 | tf_op jit(solution)/shard_map/pack_edges/pallas_call | solution.py:197
  5.2 3.9 %collective-permute-start = (f32[320,256]{1,0:T(8,128)}, f32[320,256]{1,0:T(8,128)S(1)}, u32[]{:S(2)}, u32[]{:S(2)}) collective-permute-start(f32[320,256]{1,0:T(8,128)} %get-tuple-element.29), channel_id=1, source_target_pairs={{0,32},{32,64},{64,96},{96,128},{128,160},{160,192},{192,224},{224... | collective-permute-start | bytes 983048 | tf_op jit(solution)/shard_map/ppermute | solution.py:519
  9.1 1.9 %collective-permute-start.1 = (f32[320,256]{1,0:T(8,128)}, f32[320,256]{1,0:T(8,128)S(1)}, u32[]{:S(2)}, u32[]{:S(2)}) collective-permute-start(f32[320,256]{1,0:T(8,128)} %get-tuple-element.30), channel_id=1, source_target_pairs={{32,0},{64,32},{96,64},{128,96},{160,128},{192,160},{224,192},{256... | collective-permute-start | bytes 983048 | tf_op jit(solution)/shard_map/ppermute | solution.py:519
  11.0 1.0 %pad_dynamic-slice_fusion = s32[4,3,3,3]{2,3,1,0:T(4,128)S(1)} fusion(s32[]{:T(128)S(6)} %select_n.8, s32[]{:T(128)S(6)} %select_n.9, s32[4,3,32,16]{2,3,1,0:T(8,128)} %param.14), kind=kLoop, calls=%fused_computation.1 | loop fusion | bytes 25016 | tf_op jit(solution)/shard_map/dynamic_slice | solution.py:525
  12.0 0.2 copy.12
  12.2 0.1 reshape.12
  12.3 0.1 pad_dynamic-slice_fusion.1
  12.4 0.1 copy.11
  12.6 0.1 reshape.11
  12.7 0.1 fusion.1
  12.8 0.1 fusion
  12.9 0.1 div.14.k_ref.refs_0_
  13.0 0.1 concatenate.7.p_ref
  13.1 2.4 %matrices.1 = (bf16[192,192]{1,0:T(8,128)(2,1)S(1)}, bf16[192,240]{1,0:T(8,128)(2,1)S(1)}, bf16[4,256,256]{2,1,0:T(8,128)(2,1)S(1)}, bf16[4,256,256]{2,1,0:T(8,1...) custom-call(f32[180]{0:T(256)S(1)} %div.14.k_ref.refs_0_), custom_call_target="tpu_custom_call" | custom-call | flops 8000000 | bytes 4000000 | tf_op jit(solution)/shard_map/matrices/pallas_call | solution.py:156
  15.5 0.4 collective-permute-done.l_ref.refs_2_
  15.9 5.8 %collective-permute-done.1.r_ref.refs_3_ = f32[320,256]{1,0:T(8,128)S(1)} collective-permute-done((f32[320,256]{1,0:T(8,128)}, f32[320,256]{1,0:T(8,128)S(1)}, u32[]{:S(2)}, u32[]{:S(2)}) %collective-permute-start.1) | collective-permute-done | bytes 327712 | tf_op jit(solution)/shard_map/ppermute | solution.py:519
  21.7 11.4 %collective-permute-start.2 = (f32[216,256]{1,0:T(8,128)S(1)}, f32[216,256]{1,0:T(8,128)S(1)}, u32[]{:S(2)}, u32[]{:S(2)}) collective-permute-start(f32[216,256]{1,0:T(8,128)S(1)} %get-tuple-element.31), channel_id=1, source_target_pairs={{0,1},{1,2},{2,3},{3,4},{4,5},{5,6},{6,7},{7,8},{8,9},{9,10},{10,1... | collective-permute-start | bytes 663560 | tf_op jit(solution)/shard_map/ppermute | solution.py:519
  33.1 1.9 %collective-permute-start.3 = (f32[216,256]{1,0:T(8,128)S(1)}, f32[216,256]{1,0:T(8,128)S(1)}, u32[]{:S(2)}, u32[]{:S(2)}) collective-permute-start(f32[216,256]{1,0:T(8,128)S(1)} %get-tuple-element.32), channel_id=1, source_target_pairs={{1,0},{2,1},{3,2},{4,3},{5,4},{6,5},{7,6},{8,7},{9,8},{10,9},{11,1... | collective-permute-start | bytes 663560 | tf_op jit(solution)/shard_map/ppermute | solution.py:519
  35.0 0.0 copy-done.3
  35.1 6.4 %warp.1 = (f32[4,8,48,256]{3,2,1,0:T(8,128)S(1)}, f32[4,48,128]{2,1,0:T(8,128)S(1)}, f32[4,8,48,256]{3,2,1,0:T(8,128)S(1)}, f32[4,48,128]{2,1,0:T(8,128)S(1)}) custom-call(s32[184]{0:T(256)S(1)} %concatenate.7.p_ref, f32[4,8,64,256]{3,2,1,0:T(8,128)S(1)} %copy-done.3, f32[320,256]{1,0:T(8,128)S(1)} %collective-permute-done.l_ref.refs_2_, ...), custom_call_target="tpu_custom_call" | custom-call | flops 6000000000 | bytes 8000000 | tf_op jit(solution)/shard_map/warp/pallas_call | solution.py:344
  41.5 6.7 %inner_rows.1.refs_18_ = f32[8,64,256]{2,1,0:T(8,128)S(1)} custom-call(f32[180]{0:T(256)S(1)} %div.14.k_ref.refs_0_, f32[8,64,256]{2,1,0:T(8,128)S(1)} %copy-done.1, f32[320,256]{1,0:T(8,128)S(1)} %collective-permute-done.l_ref.refs_2_, f32[320,256]{1,0:T(8,128)S(1)} %collective-permute-done.1.r_ref.refs_3_, ...), custom_call_target="tpu_custom_call" | custom-call | flops 6000000000 | bytes 12000000 | tf_op jit(solution)/shard_map/inner_rows/pallas_call | solution.py:492
  48.2 0.0 collective-permute-done.2.refs_4_
  48.2 0.0 collective-permute-done.3.refs_5_
  48.2 6.8 %edge_rows.1 = (f32[8,64,256]{2,1,0:T(8,128)S(1)}, f32[8,24,256]{2,1,0:T(8,128)S(1)}, f32[8,24,256]{2,1,0:T(8,128)S(1)}) custom-call(f32[180]{0:T(256)S(1)} %div.14.k_ref.refs_0_, f32[8,64,256]{2,1,0:T(8,128)S(1)} %copy-done.1, f32[320,256]{1,0:T(8,128)S(1)} %collective-permute-done.l_ref.refs_2_, f32[320,256]{1,0:T(8,128)S(1)} %collective-permute-done.1.r_ref.refs_3_, ...), custom_call_target="tpu_custom_call" | custom-call | flops 6000000000 | bytes 12000000 | tf_op jit(solution)/shard_map/edge_rows/pallas_call | solution.py:492
  55.1 7.6 %collective-permute-start.4 = (f32[8,24,256]{2,1,0:T(8,128)S(1)}, f32[8,24,256]{2,1,0:T(8,128)S(1)}, u32[]{:S(2)}, u32[]{:S(2)}) collective-permute-start(f32[8,24,256]{2,1,0:T(8,128)S(1)} %get-tuple-element.51), channel_id=1, source_target_pairs={{0,1},{1,2},{2,3},{3,4},{4,5},{5,6},{6,7},{7,8},{8,9},{9,10},{10,1... | collective-permute-start | bytes 589832 | tf_op jit(solution)/shard_map/ppermute | solution.py:519
  62.6 1.9 %collective-permute-start.5 = (f32[8,24,256]{2,1,0:T(8,128)S(1)}, f32[8,24,256]{2,1,0:T(8,128)S(1)}, u32[]{:S(2)}, u32[]{:S(2)}) collective-permute-start(f32[8,24,256]{2,1,0:T(8,128)S(1)} %get-tuple-element.52), channel_id=1, source_target_pairs={{1,0},{2,1},{3,2},{4,3},{5,4},{6,5},{7,6},{8,7},{9,8},{10,9},{11,1... | collective-permute-start | bytes 589832 | tf_op jit(solution)/shard_map/ppermute | solution.py:519
  64.6 0.7 collective-permute-done.4
  65.2 12.0 %collective-permute-done.5 = f32[8,24,256]{2,1,0:T(8,128)S(1)} collective-permute-done((f32[8,24,256]{2,1,0:T(8,128)S(1)}, f32[8,24,256]{2,1,0:T(8,128)S(1)}, u32[]{:S(2)}, u32[]{:S(2)}) %collective-permute-start.5) | collective-permute-done | bytes 196640 | tf_op jit(solution)/shard_map/ppermute | solution.py:519
  77.2 0.9 %multiply_multiply_fusion = f32[8,64,256]{2,1,0:T(8,128)} fusion(f32[8,64,256]{2,1,0:T(8,128)S(1)} %copy-done.1, f32[8,24,256]{2,1,0:T(8,128)S(1)} %collective-permute-done.5, f32[8,64,256]{2,1,0:T(8,128)S(1)} %get-tuple-element.50, f32[8,24,256]{2,1,0:T(8,128)S(1)} %collective-permute-done.4), kind=kLoop, calls=%fused_computation | loop fusion | flops 524288 | bytes 1966080 | tf_op jit(solution)/shard_map/mul | solution.py:548
  (15 shorter events, 0.1 us)
Async XLA Ops:
  0.0 1.0 %copy-start = (f32[8,64,256]{2,1,0:T(8,128)S(1)}, f32[8,64,256]{2,1,0:T(8,128)}, u32[]{:S(2)}) copy-start(f32[8,64,256]{2,1,0:T(8,128)} %refs_1_.3) | copy-start | bytes 1572868
  1.0 1.6 %copy-start.2 = (f32[4,8,64,256]{3,2,1,0:T(8,128)S(1)}, f32[4,8,64,256]{3,2,1,0:T(8,128)}, u32[]{:S(2)}) copy-start(f32[4,8,64,256]{3,2,1,0:T(8,128)} %v_ref.3) | copy-start | bytes 6291460
  2.6 9.7 %copy-start.4 = (s32[4,2,32,16]{2,3,1,0:T(8,128)S(1)}, s32[4,2,32,16]{2,3,1,0:T(8,128)}, u32[]{:S(2)}) copy-start(s32[4,2,32,16]{2,3,1,0:T(8,128)} %param.13) | copy-start | bytes 49156
  2.6 10.0 %copy-start.5 = (f32[4,15]{1,0:T(4,128)S(1)}, f32[4,15]{1,0:T(4,128)}, u32[]{:S(2)}) copy-start(f32[4,15]{1,0:T(4,128)} %param.12) | copy-start | bytes 724
  2.6 10.1 %copy-start.6 = (f32[4,15]{1,0:T(4,128)S(1)}, f32[4,15]{1,0:T(4,128)}, u32[]{:S(2)}) copy-start(f32[4,15]{1,0:T(4,128)} %param.11) | copy-start | bytes 724
  2.6 10.1 %copy-start.7 = (f32[4,15]{1,0:T(4,128)S(1)}, f32[4,15]{1,0:T(4,128)}, u32[]{:S(2)}) copy-start(f32[4,15]{1,0:T(4,128)} %param.10) | copy-start | bytes 724
  2.6 10.4 %copy-start.8 = (s32[2]{0:T(128)S(1)}, s32[2]{0:T(128)}, u32[]{:S(2)}) copy-start(s32[2]{0:T(128)} %constant.22.clone) | copy-start | bytes 28
  2.7 19.0 %copy-start.1 = (f32[8,64,256]{2,1,0:T(8,128)S(1)}, f32[8,64,256]{2,1,0:T(8,128)}, u32[]{:S(2)}) copy-start(f32[8,64,256]{2,1,0:T(8,128)} %refs_1_.3) | copy-start | bytes 1572868
  2.7 32.4 %copy-start.3 = (f32[4,8,64,256]{3,2,1,0:T(8,128)S(1)}, f32[4,8,64,256]{3,2,1,0:T(8,128)}, u32[]{:S(2)}) copy-start(f32[4,8,64,256]{3,2,1,0:T(8,128)} %v_ref.3) | copy-start | bytes 6291460
  5.2 10.7 %collective-permute-start = (f32[320,256]{1,0:T(8,128)}, f32[320,256]{1,0:T(8,128)S(1)}, u32[]{:S(2)}, u32[]{:S(2)}) collective-permute-start(f32[320,256]{1,0:T(8,128)} %get-tuple-element.29), channel_id=1, source_target_pairs={{0,32},{32,64},{64,96},{96,128},{128,160},{160,192},{192,224},{224... | collective-permute-start | bytes 983048 | tf_op jit(solution)/shard_map/ppermute | solution.py:519
  9.1 12.5 %collective-permute-start.1 = (f32[320,256]{1,0:T(8,128)}, f32[320,256]{1,0:T(8,128)S(1)}, u32[]{:S(2)}, u32[]{:S(2)}) collective-permute-start(f32[320,256]{1,0:T(8,128)} %get-tuple-element.30), channel_id=1, source_target_pairs={{32,0},{64,32},{96,64},{128,96},{160,128},{192,160},{224,192},{256... | collective-permute-start | bytes 983048 | tf_op jit(solution)/shard_map/ppermute | solution.py:519
  21.7 26.6 %collective-permute-start.2 = (f32[216,256]{1,0:T(8,128)S(1)}, f32[216,256]{1,0:T(8,128)S(1)}, u32[]{:S(2)}, u32[]{:S(2)}) collective-permute-start(f32[216,256]{1,0:T(8,128)S(1)} %get-tuple-element.31), channel_id=1, source_target_pairs={{0,1},{1,2},{2,3},{3,4},{4,5},{5,6},{6,7},{7,8},{8,9},{9,10},{10,1... | collective-permute-start | bytes 663560 | tf_op jit(solution)/shard_map/ppermute | solution.py:519
  33.1 15.1 %collective-permute-start.3 = (f32[216,256]{1,0:T(8,128)S(1)}, f32[216,256]{1,0:T(8,128)S(1)}, u32[]{:S(2)}, u32[]{:S(2)}) collective-permute-start(f32[216,256]{1,0:T(8,128)S(1)} %get-tuple-element.32), channel_id=1, source_target_pairs={{1,0},{2,1},{3,2},{4,3},{5,4},{6,5},{7,6},{8,7},{9,8},{10,9},{11,1... | collective-permute-start | bytes 663560 | tf_op jit(solution)/shard_map/ppermute | solution.py:519
  55.1 10.2 %collective-permute-start.4 = (f32[8,24,256]{2,1,0:T(8,128)S(1)}, f32[8,24,256]{2,1,0:T(8,128)S(1)}, u32[]{:S(2)}, u32[]{:S(2)}) collective-permute-start(f32[8,24,256]{2,1,0:T(8,128)S(1)} %get-tuple-element.51), channel_id=1, source_target_pairs={{0,1},{1,2},{2,3},{3,4},{4,5},{5,6},{6,7},{7,8},{8,9},{9,10},{10,1... | collective-permute-start | bytes 589832 | tf_op jit(solution)/shard_map/ppermute | solution.py:519
  62.6 14.6 %collective-permute-start.5 = (f32[8,24,256]{2,1,0:T(8,128)S(1)}, f32[8,24,256]{2,1,0:T(8,128)S(1)}, u32[]{:S(2)}, u32[]{:S(2)}) collective-permute-start(f32[8,24,256]{2,1,0:T(8,128)S(1)} %get-tuple-element.52), channel_id=1, source_target_pairs={{1,0},{2,1},{3,2},{4,3},{5,4},{6,5},{7,6},{8,7},{9,8},{10,9},{11,1... | collective-permute-start | bytes 589832 | tf_op jit(solution)/shard_map/ppermute | solution.py:519

commit v2 on v1

--- a/solution.py
+++ b/solution.py
@@ -21,9 +21,6 @@
 VMEM = pl.BlockSpec(memory_space=pltpu.VMEM)
 
 
-EDGES = pl.BlockSpec((ROWS, COLS), lambda *g: (VIEWS, 0))
-
-
 def limit(mib):
     return pltpu.CompilerParams(vmem_limit_bytes=mib << 20)
 
@@ -58,6 +55,10 @@
 
 def strip_col(lane):
     return jnp.where(lane < 8, lane - 8, jnp.where(lane < 16, lane + 248, 4096))
+
+
+def roll(value, by):
+    return pltpu.roll(value, by % 128, 1) if by % 128 else value
 
 
 def split(value):
@@ -165,42 +166,31 @@
 
 
 def pack_edges_kernel(e_ref, v_ref, left_ref, right_ref):
-    def fill(ref, count, width, base, lanes):
-        lane = iota((ROWS, 128), 1) // width
+    lane = iota((ROWS, 128), 1)
+    for half in range(2):
         left = jnp.zeros((ROWS, 128), F32)
         right = jnp.zeros((ROWS, 128), F32)
-        for q in range(count):
-            a, b = ref(base + q, slice(0, 128)), ref(base + q, slice(128, 256))
-            turn = (q * width + width) % 128
-            a = pltpu.roll(a, q * width, 1) if q else a
-            b = pltpu.roll(b, turn, 1) if turn else b
-            left = jnp.where(lane == q, a, left)
-            right = jnp.where(lane == q, b, right)
-        left_ref[:, lanes] = left
-        right_ref[:, lanes] = right
-
-    @pl.when(pl.program_id(0) < VIEWS)
-    def _():
-        for half in range(2):
-            fill(lambda z, cols: v_ref[0, z, :, cols], 4, 24, half * 4, slice(half * 128, half * 128 + 128))
-
-    @pl.when(pl.program_id(0) == VIEWS)
-    def _():
-        fill(lambda z, cols: e_ref[z, :, cols], Z, 16, 0, slice(0, 128))
-        for ref in (left_ref, right_ref):
-            ref[:, 128:256] = jnp.zeros((ROWS, 128), F32)
+        pieces = [(v_ref[0, half * 4 + q], q * 24, 24) for q in range(4)]
+        if half == 0:
+            pieces += [(e_ref[q], 96 + q * 16, 16) for q in range(2)]
+        for plane, at, width in pieces:
+            inside = (lane >= at) & (lane < at + width)
+            left = jnp.where(inside, roll(plane[:, 0:128], at), left)
+            right = jnp.where(inside, roll(plane[:, 128:256], at + width), right)
+        left_ref[:, half * 128 : half * 128 + 128] = left
+        right_ref[:, half * 128 : half * 128 + 128] = right
 
 
 def pack_edges(estimate, views):
-    out = jax.ShapeDtypeStruct(((VIEWS + 1) * ROWS, COLS), F32)
-    spec = pl.BlockSpec((ROWS, COLS), lambda g: (g, 0))
+    out = jax.ShapeDtypeStruct((VIEWS * ROWS, COLS), F32)
+    spec = pl.BlockSpec((ROWS, COLS), lambda v: (v, 0))
     return pl.pallas_call(
         pack_edges_kernel,
-        grid=(VIEWS + 1,),
+        grid=(VIEWS,),
         out_shape=[out, out],
         in_specs=[
-            pl.BlockSpec((Z, ROWS, COLS), lambda g: (0, 0, 0)),
-            pl.BlockSpec((1, Z, ROWS, COLS), lambda g: (jnp.minimum(g, VIEWS - 1), 0, 0, 0)),
+            pl.BlockSpec((2, ROWS, COLS), lambda v: (v, 0, 0)),
+            pl.BlockSpec((1, Z, ROWS, COLS), lambda v: (v, 0, 0, 0)),
         ],
         out_specs=[spec, spec],
         name="pack_edges",
@@ -209,21 +199,28 @@
     )(estimate, views)
 
 
-def pack_rows_kernel(e_ref, l_ref, r_ref, first_ref, last_ref):
+def pack_rows_kernel(e_ref, l_ref, r_ref, first_ref, last_ref, sides_ref):
+    lane = iota((ROWS, 128), 1) // 32
+    for ref, cols in ((l_ref, slice(0, 128)), (r_ref, slice(128, 256))):
+        side = roll(ref[0:ROWS, 0:128], -96)
+        for v in range(1, VIEWS):
+            part = roll(ref[v * ROWS : (v + 1) * ROWS, 0:128], 32 * v - 96)
+            side = jnp.where(lane == v, part, side)
+        sides_ref[:, cols] = side
+        first_ref[Z * EDGE :, cols] = side[0:EDGE]
+        last_ref[Z * EDGE :, cols] = side[ROWS - EDGE :]
     for out_ref, start in ((first_ref, 0), (last_ref, ROWS - EDGE)):
         for z in range(Z):
             out_ref[z * EDGE : (z + 1) * EDGE, :] = e_ref[z, start : start + EDGE, :]
-        out_ref[Z * EDGE :, 0:128] = l_ref[start : start + EDGE, 0:128]
-        out_ref[Z * EDGE :, 128:256] = r_ref[start : start + EDGE, 0:128]
 
 
 def pack_rows(estimate, left, right):
+    rows = jax.ShapeDtypeStruct(((Z + 1) * EDGE, COLS), F32)
     return pl.pallas_call(
         pack_rows_kernel,
-        out_shape=[jax.ShapeDtypeStruct(((Z + 1) * EDGE, COLS), F32)] * 2,
-        in_specs=[VMEM, EDGES, EDGES],
-        out_specs=[VMEM] * 2,
-        grid=(1,),
+        out_shape=[rows, rows, jax.ShapeDtypeStruct((ROWS, COLS), F32)],
+        in_specs=[VMEM] * 3,
+        out_specs=[VMEM] * 3,
         name="pack_rows",
         compiler_params=limit(12),
     )(estimate, left, right)
@@ -362,8 +359,8 @@
 
 def main_kernel(inner, *refs):
     refs = list(refs)
-    k_ref, e_ref, l_ref, r_ref = refs[:4]
-    refs = refs[4:]
+    k_ref, e_ref, sides_ref = refs[:3]
+    refs = refs[3:]
     if not inner:
         above, below = refs[:2]
         refs = refs[2:]
@@ -372,7 +369,7 @@
     if inner:
         out_refs, refs = refs[:1], refs[1:]
     else:
-        partial_ref, out_refs, refs = refs[0], refs[1:4], refs[4:]
+        out_refs, refs = refs[:3], refs[3:]
     d, g_hi, g_lo, g_t, cen, q_hi, q_lo, q_t, x2 = refs
     count = estimate_rows(inner)
     lane = iota((count, 128), 1)
@@ -380,7 +377,7 @@
     for z in range(Z):
         if inner:
             c0, c1 = e_ref[z, :, 0:128], e_ref[z, :, 128:256]
-            lh, rh = l_ref[:, 0:128], r_ref[:, 0:128]
+            lh, rh = sides_ref[:, 0:128], sides_ref[:, 128:256]
         else:
             edge = slice(z * EDGE, (z + 1) * EDGE)
             tail = slice(Z * EDGE, (Z + 1) * EDGE)
@@ -392,9 +389,9 @@
             c0 = rows(slice(0, 128), e_ref[z, :, 0:128])
             c1 = rows(slice(128, 256), e_ref[z, :, 128:256])
             lh = jnp.concatenate(
-                [above[tail, 0:128], l_ref[0:16, 0:128], l_ref[48:64, 0:128], below[tail, 0:128]], axis=0)
+                [above[tail, 0:128], sides_ref[0:16, 0:128], sides_ref[48:64, 0:128], below[tail, 0:128]], axis=0)
             rh = jnp.concatenate(
-                [above[tail, 128:256], r_ref[0:16, 0:128], r_ref[48:64, 0:128], below[tail, 128:256]], axis=0)
+                [above[tail, 128:256], sides_ref[0:16, 128:256], sides_ref[48:64, 128:256], below[tail, 128:256]], axis=0)
         lh = pltpu.roll(lh, (128 - z * 16) % 128, 1) if z else lh
         rh = pltpu.roll(rh, (128 + 16 - z * 16) % 128, 1) if z != 1 else rh
         h = jnp.where(lane < 16, lh, jnp.where(lane < 32, rh, jnp.where(
@@ -480,7 +477,7 @@
         if inner:
             out_refs[0][z] = out
         else:
-            out_refs[0][z] = out[0:64] + partial_ref[z]
+            out_refs[0][z] = out[0:64]
             out_refs[1][z] = out[64:88]
             out_refs[2][z] = out[88:112]
 
@@ -493,7 +490,7 @@
         functools.partial(main_kernel, inner),
         out_shape=[own] if inner else [own, edge, edge],
         grid=(1,),
-        in_specs=[SMEM, VMEM, EDGES, EDGES] + [VMEM] * (len(args) - 4),
+        in_specs=[SMEM] + [VMEM] * (len(args) - 1),
         out_specs=[VMEM] * (1 if inner else 3),
         scratch_shapes=[
             pltpu.VMEM((3 * estimate_rows(inner), 384), BF16),
@@ -535,15 +532,16 @@
     left, right = shifted(*pack_edges(estimate, views), "gx")
     mats = matrices(kernels)
     ly_i, ly_o, *x_mats, m_i, n_i, m_o, n_o = mats
-    above, below = shifted(*pack_rows(estimate, left, right), "gy")
+    first, last, sides = pack_rows(estimate, left, right)
+    above, below = shifted(first, last, "gy")
     w_i, s_i, w_o, s_o = warp(params, views, left, right)
-    (inside,) = main(True, kernels, estimate, left, right, w_i, s_i, ly_i, *x_mats, m_i, n_i)
     own, up, down = main(
-        False, kernels, estimate, left, right, above, below, w_o, s_o, ly_o, *x_mats,
-        m_o, n_o, inside)
+        False, kernels, estimate, sides, above, below, w_o, s_o, ly_o, *x_mats, m_o, n_o)
+    w_i, own, up, down = lax.optimization_barrier((w_i, own, up, down))
+    (inside,) = main(True, kernels, estimate, sides, w_i, s_i, ly_i, *x_mats, m_i, n_i)
     from_above, from_below = shifted(up, down, "gy")
     rest = ROWS - EDGE
-    total = own + jnp.pad(from_above, ((0, 0), (0, rest), (0, 0)))
+    total = own + inside + jnp.pad(from_above, ((0, 0), (0, rest), (0, 0)))
     total = total + jnp.pad(from_below, ((0, 0), (rest, 0), (0, 0)))
     return estimate * (total * 0.25)
 

time: 78.5 us -> 71.7 us (0.913)
  the two profiles are of different devices: /device:TPU:39 before, /device:TPU:7 now
where the time goes in v2:
time: 71.7 us; the launch traced here: 71.3 us
  Pallas kernels  24.2 us (34%)
  starting transfers between devices  23.7 us (33%)
  waiting for transfers between devices  16.3 us (23%)
  local copies, waits for them, and re-layouts  4.38 us (6%)
  other arithmetic  2.55 us (4%)
    ppermute x6, starting transfers between devices, shifted(): return (lax.ppermute(last, axis, up), lax.ppermute(first, axis, down))  23.7 us
    ppermute x6, waiting for transfers between devices, shifted(): return (lax.ppermute(last, axis, up), lax.ppermute(first, axis, down))  16.3 us
    pallas_call x2, Pallas kernels, main(): pl.pallas_call(functools.partial(main_kernel, inner), out_shape=[own] if...  13.3 us
    pallas_call x1, Pallas kernels, warp(): pl.pallas_call(warp_kernel, grid=(VIEWS,), out_shape=[w, s, w, s], in_spe...  6.48 us
    unnamed x12, local copies, waits for them, and re-layouts  2.65 us
    pallas_call x1, Pallas kernels, matrices(): pl.pallas_call(matrices_kernel, out_shape=[jax.ShapeDtypeStruct(s, BF16)...  2.39 us
    pallas_call x1, Pallas kernels, pack_edges(): pl.pallas_call(pack_edges_kernel, grid=(VIEWS,), out_shape=[out, out], in...  1.93 us
  transfers between devices with their start and end apart: 6, of which 3 were waited for; matrix products, arithmetic and copies ran while one was open for 5% of the time, Pallas kernels for 22%

profile of v2, /device:TPU:7, one launch (start us, length us, event | category | flops | bytes accessed | tf_op | source)
XLA Modules:
  0.0 71.3 jit_solution(5097989098776445398)
XLA Ops:
  0.0 1.0 %copy-done = f32[8,64,256]{2,1,0:T(8,128)S(1)} copy-done((f32[8,64,256]{2,1,0:T(8,128)S(1)}, f32[8,64,256]{2,1,0:T(8,128)}, u32[]{:S(2)}) %copy-start) | copy-done | bytes 524312
  1.0 1.6 %copy-done.2 = f32[4,8,64,256]{3,2,1,0:T(8,128)S(1)} copy-done((f32[4,8,64,256]{3,2,1,0:T(8,128)S(1)}, f32[4,8,64,256]{3,2,1,0:T(8,128)}, u32[]{:S(2)}) %copy-start.2) | copy-done | bytes 2097176
  2.6 1.9 %pack_edges.1 = (f32[256,256]{1,0:T(8,128)S(1)}, f32[256,256]{1,0:T(8,128)}) custom-call(f32[8,64,256]{2,1,0:T(8,128)S(1)} %copy-done, f32[4,8,64,256]{3,2,1,0:T(8,128)S(1)} %copy-done.2), custom_call_target="tpu_custom_call" | custom-call | flops 1000000 | bytes 3200000 | tf_op jit(solution)/shard_map/pack_edges/pallas_call | solution.py:187
  4.6 3.9 %collective-permute-start = (f32[256,256]{1,0:T(8,128)}, f32[256,256]{1,0:T(8,128)S(1)}, u32[]{:S(2)}, u32[]{:S(2)}) collective-permute-start(f32[256,256]{1,0:T(8,128)} %get-tuple-element.34), channel_id=1, source_target_pairs={{0,32},{32,64},{64,96},{96,128},{128,160},{160,192},{192,224},{224... | collective-permute-start | bytes 786440 | tf_op jit(solution)/shard_map/ppermute | solution.py:516
  8.5 1.9 %collective-permute-start.1 = (f32[256,256]{1,0:T(8,128)S(1)}, f32[256,256]{1,0:T(8,128)S(1)}, u32[]{:S(2)}, u32[]{:S(2)}) collective-permute-start(f32[256,256]{1,0:T(8,128)S(1)} %get-tuple-element.35), channel_id=1, source_target_pairs={{32,0},{64,32},{96,64},{128,96},{160,128},{192,160},{224,192},{256... | collective-permute-start | bytes 786440 | tf_op jit(solution)/shard_map/ppermute | solution.py:516
  10.4 0.8 %fusion.1 = f32[12]{0:T(128)S(1)} fusion(f32[4,15]{1,0:T(4,128)} %param.12, f32[4,15]{1,0:T(4,128)} %param.11, f32[4,15]{1,0:T(4,128)} %param.10), kind=kLoop, calls=%fused_computation.5 | loop fusion | flops 528 | bytes 768 | tf_op jit(solution)/shard_map/reduce_sum | solution.py:528
  11.2 0.8 %fusion = f32[12,15]{1,0:T(8,128)S(1)} fusion(f32[4,15]{1,0:T(4,128)} %param.12, f32[4,15]{1,0:T(4,128)} %param.11, f32[4,15]{1,0:T(4,128)} %param.10, f32[12]{0:T(128)S(1)} %fusion.1), kind=kLoop, calls=%fused_computation.4 | loop fusion | flops 540 | bytes 1488 | tf_op jit(solution)/shard_map/div | solution.py:528
  12.0 0.1 div.14.k_ref.refs_0_
  12.1 0.9 %pad_dynamic-slice_fusion.1 = s32[4,2,3,3]{2,3,1,0:T(4,128)S(1)} fusion(s32[]{:T(128)S(6)} %select_n.8, s32[]{:T(128)S(6)} %select_n.9, s32[4,2,32,16]{2,3,1,0:T(8,128)} %param.13), kind=kLoop, calls=%fused_computation.2 | loop fusion | bytes 16680 | tf_op jit(solution)/shard_map/dynamic_slice | solution.py:522
  13.1 0.1 copy.11
  13.2 0.1 reshape.11
  13.3 0.0 copy-done.4
  13.3 0.1 pad_dynamic-slice_fusion
  13.4 0.2 copy.12
  13.6 0.1 reshape.12
  13.7 0.1 concatenate.6.p_ref
  13.8 2.4 %matrices.1 = (bf16[192,192]{1,0:T(8,128)(2,1)S(1)}, bf16[192,240]{1,0:T(8,128)(2,1)S(1)}, bf16[4,256,256]{2,1,0:T(8,128)(2,1)S(1)}, bf16[4,256,256]{2,1,0:T(8,1...) custom-call(f32[180]{0:T(256)S(1)} %div.14.k_ref.refs_0_), custom_call_target="tpu_custom_call" | custom-call | flops 8000000 | bytes 4000000 | tf_op jit(solution)/shard_map/matrices/pallas_call | solution.py:157
  16.2 0.0 collective-permute-done.l_ref
  16.2 3.2 %collective-permute-done.1.r_ref = f32[256,256]{1,0:T(8,128)S(1)} collective-permute-done((f32[256,256]{1,0:T(8,128)S(1)}, f32[256,256]{1,0:T(8,128)S(1)}, u32[]{:S(2)}, u32[]{:S(2)}) %collective-permute-start.1) | collective-permute-done | bytes 262176 | tf_op jit(solution)/shard_map/ppermute | solution.py:516
  19.4 0.1 pack_rows.1
  19.5 11.4 %collective-permute-start.2 = (f32[216,256]{1,0:T(8,128)S(1)}, f32[216,256]{1,0:T(8,128)S(1)}, u32[]{:S(2)}, u32[]{:S(2)}) collective-permute-start(f32[216,256]{1,0:T(8,128)S(1)} %get-tuple-element.38), channel_id=1, source_target_pairs={{0,1},{1,2},{2,3},{3,4},{4,5},{5,6},{6,7},{7,8},{8,9},{9,10},{10,1... | collective-permute-start | bytes 663560 | tf_op jit(solution)/shard_map/ppermute | solution.py:516
  31.0 1.9 %collective-permute-start.3 = (f32[216,256]{1,0:T(8,128)S(1)}, f32[216,256]{1,0:T(8,128)S(1)}, u32[]{:S(2)}, u32[]{:S(2)}) collective-permute-start(f32[216,256]{1,0:T(8,128)S(1)} %get-tuple-element.39), channel_id=1, source_target_pairs={{1,0},{2,1},{3,2},{4,3},{5,4},{6,5},{7,6},{8,7},{9,8},{10,9},{11,1... | collective-permute-start | bytes 663560 | tf_op jit(solution)/shard_map/ppermute | solution.py:516
  32.9 6.5 %warp.1 = (f32[4,8,48,256]{3,2,1,0:T(8,128)S(1)}, f32[4,48,128]{2,1,0:T(8,128)S(1)}, f32[4,8,48,256]{3,2,1,0:T(8,128)S(1)}, f32[4,48,128]{2,1,0:T(8,128)S(1)}) custom-call(s32[184]{0:T(256)S(1)} %concatenate.6.p_ref, f32[4,8,64,256]{3,2,1,0:T(8,128)S(1)} %copy-done.3, f32[256,256]{1,0:T(8,128)S(1)} %collective-permute-done.l_ref, ...), custom_call_target="tpu_custom_call" | custom-call | flops 6000000000 | bytes 8000000 | tf_op jit(solution)/shard_map/warp/pallas_call | solution.py:341
  39.4 0.0 collective-permute-done.2.refs_3_
  39.4 7.4 %collective-permute-done.3.refs_4_ = f32[216,256]{1,0:T(8,128)S(1)} collective-permute-done((f32[216,256]{1,0:T(8,128)S(1)}, f32[216,256]{1,0:T(8,128)S(1)}, u32[]{:S(2)}, u32[]{:S(2)}) %collective-permute-start.3) | collective-permute-done | bytes 221216 | tf_op jit(solution)/shard_map/ppermute | solution.py:516
  46.8 6.7 %edge_rows.1 = (f32[8,64,256]{2,1,0:T(8,128)S(1)}, f32[8,24,256]{2,1,0:T(8,128)S(1)}, f32[8,24,256]{2,1,0:T(8,128)S(1)}) custom-call(f32[180]{0:T(256)S(1)} %div.14.k_ref.refs_0_, f32[8,64,256]{2,1,0:T(8,128)S(1)} %copy-done.1, f32[64,256]{1,0:T(8,128)S(1)} %get-tuple-element.37.refs_2_, f32[216,256]{1,0:T(8,128)S(1)} %collective-permute-done.2.refs_3_, ...), custom_call_target="tpu_custom_call" | custom-call | flops 6000000000 | bytes 12000000 | tf_op jit(solution)/shard_map/edge_rows/pallas_call | solution.py:489
  53.5 1.9 %collective-permute-start.4 = (f32[8,24,256]{2,1,0:T(8,128)S(1)}, f32[8,24,256]{2,1,0:T(8,128)S(1)}, u32[]{:S(2)}, u32[]{:S(2)}) collective-permute-start(f32[8,24,256]{2,1,0:T(8,128)S(1)} %get-tuple-element.61), channel_id=1, source_target_pairs={{0,1},{1,2},{2,3},{3,4},{4,5},{5,6},{6,7},{7,8},{8,9},{9,10},{10,1... | collective-permute-start | bytes 589832 | tf_op jit(solution)/shard_map/ppermute | solution.py:516
  55.4 2.6 %collective-permute-start.5 = (f32[8,24,256]{2,1,0:T(8,128)S(1)}, f32[8,24,256]{2,1,0:T(8,128)S(1)}, u32[]{:S(2)}, u32[]{:S(2)}) collective-permute-start(f32[8,24,256]{2,1,0:T(8,128)S(1)} %get-tuple-element.62), channel_id=1, source_target_pairs={{1,0},{2,1},{3,2},{4,3},{5,4},{6,5},{7,6},{8,7},{9,8},{10,9},{11,1... | collective-permute-start | bytes 589832 | tf_op jit(solution)/shard_map/ppermute | solution.py:516
  58.0 6.6 %inner_rows.1 = f32[8,64,256]{2,1,0:T(8,128)S(1)} custom-call(f32[180]{0:T(256)S(1)} %div.14.k_ref.refs_0_, f32[8,64,256]{2,1,0:T(8,128)S(1)} %copy-done.1, f32[64,256]{1,0:T(8,128)S(1)} %get-tuple-element.37.refs_2_, f32[4,8,48,256]{3,2,1,0:T(8,128)S(1)} %get-tuple-element.56.refs_3_, f32[4,48,128]{2,1,0:T(8,128)S(1)} %get-tuple-element.57.refs_4_, ...), custom_call_target="tpu_custom_call" | custom-call | flops 6000000000 | bytes 12000000 | tf_op jit(solution)/shard_map/inner_rows/pallas_call | solution.py:489
  64.6 0.0 collective-permute-done.4
  64.6 5.8 %collective-permute-done.5 = f32[8,24,256]{2,1,0:T(8,128)S(1)} collective-permute-done((f32[8,24,256]{2,1,0:T(8,128)S(1)}, f32[8,24,256]{2,1,0:T(8,128)S(1)}, u32[]{:S(2)}, u32[]{:S(2)}) %collective-permute-start.5) | collective-permute-done | bytes 196640 | tf_op jit(solution)/shard_map/ppermute | solution.py:516
  70.4 0.9 %multiply_multiply_fusion = f32[8,64,256]{2,1,0:T(8,128)} fusion(f32[8,64,256]{2,1,0:T(8,128)S(1)} %copy-done.1, f32[8,24,256]{2,1,0:T(8,128)S(1)} %collective-permute-done.5, f32[8,24,256]{2,1,0:T(8,128)S(1)} %collective-permute-done.4, f32[8,64,256]{2,1,0:T(8,128)S(1)} %get-tuple-element.55, f32[8,64,256]{2,1,0:T(8,128)S(1)} %inner_rows.1), kind=kLoop, calls=%fused_computation | loop fusion | flops 655360 | bytes 2490368 | tf_op jit(solution)/shard_map/mul | solution.py:546
  (9 shorter events, 0.0 us)
Async XLA Ops:
  0.0 1.0 %copy-start = (f32[8,64,256]{2,1,0:T(8,128)S(1)}, f32[8,64,256]{2,1,0:T(8,128)}, u32[]{:S(2)}) copy-start(f32[8,64,256]{2,1,0:T(8,128)} %refs_1_.3) | copy-start | bytes 1572868
  1.0 1.6 %copy-start.2 = (f32[4,8,64,256]{3,2,1,0:T(8,128)S(1)}, f32[4,8,64,256]{3,2,1,0:T(8,128)}, u32[]{:S(2)}) copy-start(f32[4,8,64,256]{3,2,1,0:T(8,128)} %v_ref.3) | copy-start | bytes 6291460
  2.6 10.7 %copy-start.4 = (s32[4,3,32,16]{2,3,1,0:T(8,128)S(1)}, s32[4,3,32,16]{2,3,1,0:T(8,128)}, u32[]{:S(2)}) copy-start(s32[4,3,32,16]{2,3,1,0:T(8,128)} %param.14) | copy-start | bytes 73732
  2.6 11.1 %copy-start.5 = (s32[2]{0:T(128)S(1)}, s32[2]{0:T(128)}, u32[]{:S(2)}) copy-start(s32[2]{0:T(128)} %constant.22.clone) | copy-start | bytes 28
  2.6 16.8 %copy-start.1 = (f32[8,64,256]{2,1,0:T(8,128)S(1)}, f32[8,64,256]{2,1,0:T(8,128)}, u32[]{:S(2)}) copy-start(f32[8,64,256]{2,1,0:T(8,128)} %refs_1_.3) | copy-start | bytes 1572868
  2.6 30.3 %copy-start.3 = (f32[4,8,64,256]{3,2,1,0:T(8,128)S(1)}, f32[4,8,64,256]{3,2,1,0:T(8,128)}, u32[]{:S(2)}) copy-start(f32[4,8,64,256]{3,2,1,0:T(8,128)} %v_ref.3) | copy-start | bytes 6291460
  4.6 11.6 %collective-permute-start = (f32[256,256]{1,0:T(8,128)}, f32[256,256]{1,0:T(8,128)S(1)}, u32[]{:S(2)}, u32[]{:S(2)}) collective-permute-start(f32[256,256]{1,0:T(8,128)} %get-tuple-element.34), channel_id=1, source_target_pairs={{0,32},{32,64},{64,96},{96,128},{128,160},{160,192},{192,224},{224... | collective-permute-start | bytes 786440 | tf_op jit(solution)/shard_map/ppermute | solution.py:516
  8.5 10.9 %collective-permute-start.1 = (f32[256,256]{1,0:T(8,128)S(1)}, f32[256,256]{1,0:T(8,128)S(1)}, u32[]{:S(2)}, u32[]{:S(2)}) collective-permute-start(f32[256,256]{1,0:T(8,128)S(1)} %get-tuple-element.35), channel_id=1, source_target_pairs={{32,0},{64,32},{96,64},{128,96},{160,128},{192,160},{224,192},{256... | collective-permute-start | bytes 786440 | tf_op jit(solution)/shard_map/ppermute | solution.py:516
  19.5 19.9 %collective-permute-start.2 = (f32[216,256]{1,0:T(8,128)S(1)}, f32[216,256]{1,0:T(8,128)S(1)}, u32[]{:S(2)}, u32[]{:S(2)}) collective-permute-start(f32[216,256]{1,0:T(8,128)S(1)} %get-tuple-element.38), channel_id=1, source_target_pairs={{0,1},{1,2},{2,3},{3,4},{4,5},{5,6},{6,7},{7,8},{8,9},{9,10},{10,1... | collective-permute-start | bytes 663560 | tf_op jit(solution)/shard_map/ppermute | solution.py:516
  31.0 15.8 %collective-permute-start.3 = (f32[216,256]{1,0:T(8,128)S(1)}, f32[216,256]{1,0:T(8,128)S(1)}, u32[]{:S(2)}, u32[]{:S(2)}) collective-permute-start(f32[216,256]{1,0:T(8,128)S(1)} %get-tuple-element.39), channel_id=1, source_target_pairs={{1,0},{2,1},{3,2},{4,3},{5,4},{6,5},{7,6},{8,7},{9,8},{10,9},{11,1... | collective-permute-start | bytes 663560 | tf_op jit(solution)/shard_map/ppermute | solution.py:516
  53.5 11.2 %collective-permute-start.4 = (f32[8,24,256]{2,1,0:T(8,128)S(1)}, f32[8,24,256]{2,1,0:T(8,128)S(1)}, u32[]{:S(2)}, u32[]{:S(2)}) collective-permute-start(f32[8,24,256]{2,1,0:T(8,128)S(1)} %get-tuple-element.61), channel_id=1, source_target_pairs={{0,1},{1,2},{2,3},{3,4},{4,5},{5,6},{6,7},{7,8},{8,9},{9,10},{10,1... | collective-permute-start | bytes 589832 | tf_op jit(solution)/shard_map/ppermute | solution.py:516
  55.4 15.0 %collective-permute-start.5 = (f32[8,24,256]{2,1,0:T(8,128)S(1)}, f32[8,24,256]{2,1,0:T(8,128)S(1)}, u32[]{:S(2)}, u32[]{:S(2)}) collective-permute-start(f32[8,24,256]{2,1,0:T(8,128)S(1)} %get-tuple-element.62), channel_id=1, source_target_pairs={{1,0},{2,1},{3,2},{4,3},{5,4},{6,5},{7,6},{8,7},{9,8},{10,9},{11,1... | collective-permute-start | bytes 589832 | tf_op jit(solution)/shard_map/ppermute | solution.py:516

commit v3 on v2

--- a/solution.py
+++ b/solution.py
@@ -6,6 +6,7 @@
 from jax.experimental import pallas as pl
 from jax.experimental.pallas import tpu as pltpu
 from jax.sharding import PartitionSpec as P
+
 
 F32 = jnp.float32
 BF16 = jnp.bfloat16
@@ -14,7 +15,8 @@
 Z = 8
 ROWS = 64
 COLS = 256
-SET = 48
+SET = 32
+NEAR = 48
 EDGE = 24
 
 SMEM = pl.BlockSpec(memory_space=pltpu.SMEM)
@@ -27,30 +29,6 @@
 
 def iota(shape, dim):
     return lax.broadcasted_iota(jnp.int32, shape, dim)
-
-
-def sample_row(inner, idx):
-    if inner:
-        return idx + 8
-    return jnp.where(
-        idx < 8, idx, jnp.where(idx < 16, idx + 48, jnp.where(idx < 32, idx - 32, idx + 32))
-    )
-
-
-def estimate_row(inner, idx):
-    return idx if inner else jnp.where(idx < 40, idx - 24, idx + 8)
-
-
-def output_row(inner, idx):
-    return idx if inner else jnp.where(idx < 64, idx, jnp.where(idx < 88, idx - 88, idx - 24))
-
-
-def estimate_rows(inner):
-    return 64 if inner else 80
-
-
-def output_rows(inner):
-    return 64 if inner else 112
 
 
 def strip_col(lane):
@@ -73,18 +51,16 @@
     return total
 
 
-def matrices_kernel(k_ref, ly_i, ly_o, f_hi, f_lo, f_t, f_s, b_hi, b_lo, b_t, m_i, n_i, m_o, n_o):
+def matrices_kernel(k_ref, ly, f_hi, f_lo, f_t, f_s, b_hi, b_lo, b_t, m_ref, n_ref):
     kx, ky = 0, VIEWS * TAPS
-    for inner, ly in ((True, ly_i), (False, ly_o)):
-        count = estimate_rows(inner)
-        shape = (SET, 3 * count)
-        lane = iota(shape, 1)
-        seg = jnp.where(lane < count, 0, jnp.where(lane < 2 * count, 1, 2))
-        differ = estimate_row(inner, lane - seg * count) - sample_row(inner, iota(shape, 0)) + 7
-        for v in range(VIEWS):
-            weight = band(k_ref, ky + v * TAPS, differ)
-            high = weight.astype(BF16).astype(F32)
-            ly[v * SET : (v + 1) * SET, :] = jnp.where(seg < 2, high, weight - high).astype(BF16)
+    shape = (SET, 3 * NEAR)
+    lane = iota(shape, 1)
+    seg = jnp.where(lane < NEAR, 0, jnp.where(lane < 2 * NEAR, 1, 2))
+    differ = lane - seg * NEAR - iota(shape, 0) - 1
+    for v in range(VIEWS):
+        weight = band(k_ref, ky + v * TAPS, differ)
+        high = weight.astype(BF16).astype(F32)
+        ly[v * SET : (v + 1) * SET, :] = jnp.where(seg < 2, high, weight - high).astype(BF16)
 
     view = iota((1, VIEWS * SET), 1) // SET
     taps = []
@@ -93,16 +69,14 @@
         for v in range(1, VIEWS):
             value = jnp.where(view == v, k_ref[ky + v * TAPS + tap], value)
         taps.append(value)
-    for inner, m_ref, n_ref in ((True, m_i, n_i), (False, m_o, n_o)):
-        shape = (output_rows(inner), VIEWS * SET)
-        lane = iota(shape, 1)
-        differ = output_row(inner, iota(shape, 0)) - sample_row(inner, lane - (lane // SET) * SET) + 7
-        weight = jnp.zeros(shape, F32)
-        for tap in range(TAPS):
-            weight = jnp.where(differ == tap, taps[tap], weight)
-        high, low = split(weight)
-        m_ref[...] = high
-        n_ref[...] = low
+    shape = (NEAR, VIEWS * SET)
+    differ = iota(shape, 0) - (iota(shape, 1) & (SET - 1)) - 1
+    weight = jnp.zeros(shape, F32)
+    for tap in range(TAPS):
+        weight = jnp.where(differ == tap, taps[tap], weight)
+    high, low = split(weight)
+    m_ref[...] = high
+    n_ref[...] = low
 
     def per_view(v, carry):
         base = kx + v * TAPS
@@ -151,8 +125,8 @@
 
 def matrices(kernels):
     shapes = [
-        (192, 192), (192, 240), (4, 256, 256), (4, 256, 256), (4, 256, 256), (4, 256, 128),
-        (4, 256, 256), (4, 256, 256), (4, 128, 256), (64, 192), (64, 192), (112, 192), (112, 192),
+        (128, 144), (4, 256, 256), (4, 256, 256), (4, 256, 256), (4, 256, 128),
+        (4, 256, 256), (4, 256, 256), (4, 128, 256), (48, 128), (48, 128),
     ]
     return pl.pallas_call(
         matrices_kernel,
@@ -234,7 +208,7 @@
     return total
 
 
-def warp_kernel(p_ref, v_ref, l_ref, r_ref, wi_ref, si_ref, wo_ref, so_ref,
+def warp_kernel(p_ref, v_ref, l_ref, r_ref, wt_ref, st_ref, wi_ref, si_ref, wb_ref, sb_ref,
                 src, c_hi, c_lo, s_hi, s_lo):
     v = pl.program_id(0)
     j, i = p_ref[180], p_ref[181]
@@ -265,12 +239,11 @@
     source = iota(shape, 1)
     upper_plane = source >= 128
     source = source & 63
-    target = jnp.where(row < 48, row + 8, jnp.where(row < 56, row - 48, jnp.where(
-        row < 64, row, jnp.where(row < 80, row - 80, row - 16))))
+    target = row - 16
 
     def rows_matrix(c):
         def pick(values):
-            return jnp.where(row < 64, values[1], jnp.where(row < 80, values[0], values[2]))
+            return jnp.where(row < 16, values[0], jnp.where(row < 80, values[1], values[2]))
 
         good_c = (i > 0) if c == 0 else ((i < p_ref[183]) if c == 2 else (i >= 0))
         good = [((j > 0) & good_c).astype(F32), good_c.astype(F32), ((j < p_ref[182]) & good_c).astype(F32)]
@@ -292,8 +265,8 @@
             (c, c_hi, c_lo, 0, 384), (s[0:96], s_hi, s_lo, 0, 128), (s[96:192], s_hi, s_lo, 128, 128)):
             high, low = split(value)
             for ref, part in ((hi_ref, high), (lo_ref, low)):
-                ref[z * 64 : z * 64 + 64, col : col + width] = part[0:64]
-                ref[512 + z * 16 : 528 + z * 16, col : col + width] = part[64:80]
+                ref[z * 64 : z * 64 + 64, col : col + width] = part[16:80]
+                ref[512 + z * 16 : 528 + z * 16, col : col + width] = part[0:16]
                 ref[640 + z * 16 : 656 + z * 16, col : col + width] = part[80:96]
 
     for b, start, count in ((1, 0, 512), (0, 512, 128), (2, 640, 128)):
@@ -318,18 +291,16 @@
         w += jnp.dot(c_lo[rows], x_map, preferred_element_type=F32)
         s = jnp.dot(s_hi[rows], s_map, preferred_element_type=F32)
         s += jnp.dot(s_lo[rows], s_map, preferred_element_type=F32)
-        at = 0 if b == 1 else (16 if b == 0 else 32)
-        for z in range(Z):
-            if b == 1:
-                wi_ref[0, z] = w[z * 64 : z * 64 + 48]
-                wo_ref[0, z, 0:16] = w[z * 64 + 48 : z * 64 + 64]
-            else:
-                wo_ref[0, z, at : at + 16] = w[z * 16 : z * 16 + 16]
+        count = count // Z
         if b == 1:
-            si_ref[0] = planes_to_lanes([s[z * 64 : z * 64 + 48] for z in range(Z)])
-            so_ref[0, 0:16] = planes_to_lanes([s[z * 64 + 48 : z * 64 + 64] for z in range(Z)])
+            places = [(wt_ref, st_ref, 16, 0, 16), (wi_ref, si_ref, 0, 16, 48), (wb_ref, sb_ref, 0, 48, 64)]
         else:
-            so_ref[0, at : at + 16] = planes_to_lanes([s[z * 16 : z * 16 + 16] for z in range(Z)])
+            places = [(wt_ref, st_ref, 0, 0, 16) if b == 0 else (wb_ref, sb_ref, 16, 0, 16)]
+        for w_ref, s_ref, at, first, last in places:
+            to = slice(at, at + last - first)
+            for z in range(Z):
+                w_ref[0, z, to] = w[z * count + first : z * count + last]
+            s_ref[0, to] = planes_to_lanes([s[z * count + first : z * count + last] for z in range(Z)])
 
 
 def warp(params, views, left, right):
@@ -341,9 +312,9 @@
     return pl.pallas_call(
         warp_kernel,
         grid=(VIEWS,),
-        out_shape=[w, s, w, s],
+        out_shape=[w, s] * 3,
         in_specs=[SMEM, pl.BlockSpec((1, Z, ROWS, COLS), lambda v: (v, 0, 0, 0)), side, side],
-        out_specs=[w_spec, s_spec, w_spec, s_spec],
+        out_specs=[w_spec, s_spec] * 3,
         scratch_shapes=[
             pltpu.VMEM((9 * 128, 384), BF16),
             pltpu.VMEM((768, 384), BF16),
@@ -357,41 +328,37 @@
     )(params, views, left, right)
 
 
-def main_kernel(inner, *refs):
+def main_kernel(mode, *refs):
     refs = list(refs)
     k_ref, e_ref, sides_ref = refs[:3]
     refs = refs[3:]
-    if not inner:
-        above, below = refs[:2]
-        refs = refs[2:]
+    if mode != "inner":
+        halo, refs = refs[0], refs[1:]
     w_ref, s_ref, ly, f_hi, f_lo, f_t, f_s, b_hi, b_lo, b_t, m_ref, n_ref = refs[:12]
     refs = refs[12:]
-    if inner:
-        out_refs, refs = refs[:1], refs[1:]
-    else:
-        out_refs, refs = refs[:3], refs[3:]
+    outs = 1 if mode == "inner" else 2
+    out_refs, refs = refs[:outs], refs[outs:]
     d, g_hi, g_lo, g_t, cen, q_hi, q_lo, q_t, x2 = refs
-    count = estimate_rows(inner)
-    lane = iota((count, 128), 1)
+    lane = iota((NEAR, 128), 1)
     lane_out = iota((VIEWS * SET, 128), 1)
     for z in range(Z):
-        if inner:
-            c0, c1 = e_ref[z, :, 0:128], e_ref[z, :, 128:256]
-            lh, rh = sides_ref[:, 0:128], sides_ref[:, 128:256]
-        else:
-            edge = slice(z * EDGE, (z + 1) * EDGE)
-            tail = slice(Z * EDGE, (Z + 1) * EDGE)
-
-            def rows(cols, own):
-                return jnp.concatenate(
-                    [above[edge, cols], own[0:16], own[48:64], below[edge, cols]], axis=0)
-
-            c0 = rows(slice(0, 128), e_ref[z, :, 0:128])
-            c1 = rows(slice(128, 256), e_ref[z, :, 128:256])
-            lh = jnp.concatenate(
-                [above[tail, 0:128], sides_ref[0:16, 0:128], sides_ref[48:64, 0:128], below[tail, 0:128]], axis=0)
-            rh = jnp.concatenate(
-                [above[tail, 128:256], sides_ref[0:16, 128:256], sides_ref[48:64, 128:256], below[tail, 128:256]], axis=0)
+        edge = slice(z * EDGE, (z + 1) * EDGE)
+        tail = slice(Z * EDGE, (Z + 1) * EDGE)
+
+        def rows(own, beside):
+            if mode == "inner":
+                return own(8, 56)
+            if mode == "top":
+                return jnp.concatenate([beside, own(0, EDGE)], axis=0)
+            return jnp.concatenate([own(ROWS - EDGE, ROWS), beside], axis=0)
+
+        def both_of(cols):
+            near = rows(lambda a, b: e_ref[z, a:b, cols], None if mode == "inner" else halo[edge, cols])
+            far = rows(lambda a, b: sides_ref[a:b, cols], None if mode == "inner" else halo[tail, cols])
+            return near, far
+
+        c0, lh = both_of(slice(0, 128))
+        c1, rh = both_of(slice(128, 256))
         lh = pltpu.roll(lh, (128 - z * 16) % 128, 1) if z else lh
         rh = pltpu.roll(rh, (128 + 16 - z * 16) % 128, 1) if z != 1 else rh
         h = jnp.where(lane < 16, lh, jnp.where(lane < 32, rh, jnp.where(
@@ -400,9 +367,9 @@
         for t, part in enumerate((c0, c1, h)):
             high, low = split(part)
             cols = slice(t * 128, t * 128 + 128)
-            d[0:count, cols] = high
-            d[count : 2 * count, cols] = low
-            d[2 * count : 3 * count, cols] = high
+            d[0:NEAR, cols] = high
+            d[NEAR : 2 * NEAR, cols] = low
+            d[2 * NEAR : 3 * NEAR, cols] = high
         y = jnp.dot(ly[...], d[...], preferred_element_type=F32)
         high = y.astype(BF16)
         low = y - high.astype(F32)
@@ -429,7 +396,7 @@
             dot(g_hi[v], f_lo[v]) + dot(g_t[v], f_t[v]))
         strip = dot(g_t[v], f_s[v])
         taps = [k_ref[2 * VIEWS * TAPS + v * TAPS + t] for t in range(TAPS)]
-        for rb in range(3):
+        for rb in range(SET // 16):
             for t in range(2):
                 cols = slice(t * 128, t * 128 + 128)
                 at = [slice(z * SET + rb * 16, z * SET + rb * 16 + 16) for z in range(Z)]
@@ -474,26 +441,24 @@
         out = jnp.dot(m_ref[...], high, preferred_element_type=F32)
         out += jnp.dot(m_ref[...], low, preferred_element_type=F32)
         out += jnp.dot(n_ref[...], high, preferred_element_type=F32)
-        if inner:
+        if mode == "inner":
             out_refs[0][z] = out
         else:
-            out_refs[0][z] = out[0:64]
-            out_refs[1][z] = out[64:88]
-            out_refs[2][z] = out[88:112]
-
-
-def main(inner, *args):
-    own = jax.ShapeDtypeStruct((Z, ROWS, COLS), F32)
-    edge = jax.ShapeDtypeStruct((Z, EDGE, COLS), F32)
+            out_refs[0][z] = out[0:EDGE]
+            out_refs[1][z] = out[EDGE:NEAR]
+
+
+def main(part, *args):
     rows = Z * SET
+    outs = 1 if part == "inner" else 2
     return pl.pallas_call(
-        functools.partial(main_kernel, inner),
-        out_shape=[own] if inner else [own, edge, edge],
+        functools.partial(main_kernel, part),
+        out_shape=[jax.ShapeDtypeStruct((Z, NEAR // outs, COLS), F32)] * outs,
         grid=(1,),
         in_specs=[SMEM] + [VMEM] * (len(args) - 1),
-        out_specs=[VMEM] * (1 if inner else 3),
+        out_specs=[VMEM] * outs,
         scratch_shapes=[
-            pltpu.VMEM((3 * estimate_rows(inner), 384), BF16),
+            pltpu.VMEM((3 * NEAR, 384), BF16),
             pltpu.VMEM((VIEWS, rows, 256), BF16),
             pltpu.VMEM((VIEWS, rows, 256), BF16),
             pltpu.VMEM((VIEWS, rows, 256), BF16),
@@ -503,17 +468,17 @@
             pltpu.VMEM((VIEWS, rows, 128), BF16),
             pltpu.VMEM((Z, 2, VIEWS, SET, COLS), BF16),
         ],
-        name="inner_rows" if inner else "edge_rows",
-        compiler_params=limit(28),
-        cost_estimate=pl.CostEstimate(flops=6_000_000_000, bytes_accessed=12_000_000, transcendentals=0),
+        compiler_params=limit(24),
+        cost_estimate=pl.CostEstimate(flops=4_000_000_000, bytes_accessed=8_000_000, transcendentals=0),
     )(*args)
 
 
-def shifted(first, last, axis):
-    count = lax.axis_size(axis)
-    up = [(i, i + 1) for i in range(count - 1)]
-    down = [(i + 1, i) for i in range(count - 1)]
-    return lax.ppermute(last, axis, up), lax.ppermute(first, axis, down)
+def from_before(value, axis):
+    return lax.ppermute(value, axis, [(i, i + 1) for i in range(lax.axis_size(axis) - 1)])
+
+
+def from_after(value, axis):
+    return lax.ppermute(value, axis, [(i + 1, i) for i in range(lax.axis_size(axis) - 1)])
 
 
 def neighbours(table, j, i):
@@ -529,20 +494,26 @@
     params = jnp.concatenate(
         [neighbours(block_offsets, j, i), neighbours(sub_shifts, j, i), j[None], i[None],
          jnp.array([lax.axis_size("gy") - 1, lax.axis_size("gx") - 1], jnp.int32)])
-    left, right = shifted(*pack_edges(estimate, views), "gx")
-    mats = matrices(kernels)
-    ly_i, ly_o, *x_mats, m_i, n_i, m_o, n_o = mats
+    first, last = pack_edges(estimate, views)
+    left, right = from_before(last, "gx"), from_after(first, "gx")
+    ly, *x_mats, m_mat, n_mat = matrices(kernels)
+    mats = (ly, *x_mats, m_mat, n_mat)
     first, last, sides = pack_rows(estimate, left, right)
-    above, below = shifted(first, last, "gy")
-    w_i, s_i, w_o, s_o = warp(params, views, left, right)
-    own, up, down = main(
-        False, kernels, estimate, sides, above, below, w_o, s_o, ly_o, *x_mats, m_o, n_o)
-    w_i, own, up, down = lax.optimization_barrier((w_i, own, up, down))
-    (inside,) = main(True, kernels, estimate, sides, w_i, s_i, ly_i, *x_mats, m_i, n_i)
-    from_above, from_below = shifted(up, down, "gy")
-    rest = ROWS - EDGE
-    total = own + inside + jnp.pad(from_above, ((0, 0), (0, rest), (0, 0)))
-    total = total + jnp.pad(from_below, ((0, 0), (rest, 0), (0, 0)))
+    below = from_after(first, "gy")
+    above = from_before(last, "gy")
+    w_t, s_t, w_i, s_i, w_b, s_b = warp(params, views, left, right)
+    bottom, down = main("bottom", kernels, estimate, sides, below, w_b, s_b, *mats)
+    from_above = from_before(down, "gy")
+    s_t, bottom, down = lax.optimization_barrier((s_t, bottom, down))
+    up, top = main("top", kernels, estimate, sides, above, w_t, s_t, *mats)
+    from_below = from_after(up, "gy")
+    s_i, up, top = lax.optimization_barrier((s_i, up, top))
+    (inner,) = main("inner", kernels, estimate, sides, w_i, s_i, *mats)
+
+    def place(value, start):
+        return jnp.pad(value, ((0, 0), (start, ROWS - start - value.shape[1]), (0, 0)))
+
+    total = place(inner, 8) + place(top + from_above, 0) + place(bottom + from_below, ROWS - EDGE)
     return estimate * (total * 0.25)
 
 

time: 71.7 us -> 73.6 us (1.026)
  Pallas kernels: 24.2 us -> 26.2 us
    pallas_call x3 -> x4, Pallas kernels: 19.8 us -> 22.3 us  [the longest x3 15.8 us: main(): pl.pallas_call(functools.partial(main_kernel, part), out_shape=[jax.Shape...]
  transfers between devices with their start and end apart: 6 -> 6, of which waited for: 3 -> 3; matrix products, arithmetic and copies ran while one was open for 5% -> 5% of each run, Pallas kernels for 22% -> 33%
where the time goes in v3:
time: 73.6 us; the launch traced here: 73.2 us
  Pallas kernels  26.2 us (36%)
  starting transfers between devices  23.7 us (32%)
  waiting for transfers between devices  16.2 us (22%)
  local copies, waits for them, and re-layouts  4.38 us (6%)
  other arithmetic  2.57 us (3%)
    ppermute x3, starting transfers between devices, from_before(): lax.ppermute(value, axis, [(i, i + 1) for i in range(lax.axis_size(axis)...  17.3 us
    ppermute x3, waiting for transfers between devices, from_after(): lax.ppermute(value, axis, [(i + 1, i) for i in range(lax.axis_size(axis)...  16.2 us
    pallas_call x3, Pallas kernels, main(): pl.pallas_call(functools.partial(main_kernel, part), out_shape=[jax.Shape...  15.8 us
    pallas_call x1, Pallas kernels, warp(): pl.pallas_call(warp_kernel, grid=(VIEWS,), out_shape=[w, s] * 3, in_specs...  6.5 us
    ppermute x3, starting transfers between devices, from_after(): lax.ppermute(value, axis, [(i + 1, i) for i in range(lax.axis_size(axis)...  6.43 us
    unnamed x12, local copies, waits for them, and re-layouts  2.65 us
    pallas_call x1, Pallas kernels, pack_edges(): pl.pallas_call(pack_edges_kernel, grid=(VIEWS,), out_shape=[out, out], in...  1.91 us
    pallas_call x1, Pallas kernels, matrices(): pl.pallas_call(matrices_kernel, out_shape=[jax.ShapeDtypeStruct(s, BF16)...  1.89 us
  transfers between devices with their start and end apart: 6, of which 3 were waited for; matrix products, arithmetic and copies ran while one was open for 5% of the time, Pallas kernels for 33%

profile of v3, /device:TPU:7, one launch (start us, length us, event | category | flops | bytes accessed | tf_op | source)
XLA Modules:
  0.0 73.2 jit_solution(11474799490594594945)
XLA Ops:
  0.0 1.0 %copy-done = f32[8,64,256]{2,1,0:T(8,128)S(1)} copy-done((f32[8,64,256]{2,1,0:T(8,128)S(1)}, f32[8,64,256]{2,1,0:T(8,128)}, u32[]{:S(2)}) %copy-start) | copy-done | bytes 524312
  1.0 1.6 %copy-done.2 = f32[4,8,64,256]{3,2,1,0:T(8,128)S(1)} copy-done((f32[4,8,64,256]{3,2,1,0:T(8,128)S(1)}, f32[4,8,64,256]{3,2,1,0:T(8,128)}, u32[]{:S(2)}) %copy-start.2) | copy-done | bytes 2097176
  2.6 1.9 %pack_edges.1 = (f32[256,256]{1,0:T(8,128)S(1)}, f32[256,256]{1,0:T(8,128)}) custom-call(f32[8,64,256]{2,1,0:T(8,128)S(1)} %copy-done, f32[4,8,64,256]{3,2,1,0:T(8,128)S(1)} %copy-done.2), custom_call_target="tpu_custom_call" | custom-call | flops 1000000 | bytes 3200000 | tf_op jit(solution)/shard_map/pack_edges/pallas_call | solution.py:161
  4.6 3.9 %collective-permute-start = (f32[256,256]{1,0:T(8,128)}, f32[256,256]{1,0:T(8,128)S(1)}, u32[]{:S(2)}, u32[]{:S(2)}) collective-permute-start(f32[256,256]{1,0:T(8,128)} %get-tuple-element.34), channel_id=1, source_target_pairs={{0,32},{32,64},{64,96},{96,128},{128,160},{160,192},{192,224},{224... | collective-permute-start | bytes 786440 | tf_op jit(solution)/shard_map/ppermute | solution.py:477
  8.5 1.9 %collective-permute-start.1 = (f32[256,256]{1,0:T(8,128)S(1)}, f32[256,256]{1,0:T(8,128)S(1)}, u32[]{:S(2)}, u32[]{:S(2)}) collective-permute-start(f32[256,256]{1,0:T(8,128)S(1)} %get-tuple-element.35), channel_id=1, source_target_pairs={{32,0},{64,32},{96,64},{128,96},{160,128},{192,160},{224,192},{256... | collective-permute-start | bytes 786440 | tf_op jit(solution)/shard_map/ppermute | solution.py:481
  10.4 0.8 %fusion.1 = f32[12]{0:T(128)S(1)} fusion(f32[4,15]{1,0:T(4,128)} %param.12, f32[4,15]{1,0:T(4,128)} %param.11, f32[4,15]{1,0:T(4,128)} %param.10), kind=kLoop, calls=%fused_computation.5 | loop fusion | flops 528 | bytes 768 | tf_op jit(solution)/shard_map/reduce_sum | solution.py:493
  11.2 0.8 %fusion = f32[12,15]{1,0:T(8,128)S(1)} fusion(f32[4,15]{1,0:T(4,128)} %param.12, f32[4,15]{1,0:T(4,128)} %param.11, f32[4,15]{1,0:T(4,128)} %param.10, f32[12]{0:T(128)S(1)} %fusion.1), kind=kLoop, calls=%fused_computation.4 | loop fusion | flops 540 | bytes 1488 | tf_op jit(solution)/shard_map/div | solution.py:493
  12.0 0.1 div.14.k_ref.refs_0_
  12.1 0.9 %pad_dynamic-slice_fusion.1 = s32[4,2,3,3]{2,3,1,0:T(4,128)S(1)} fusion(s32[]{:T(128)S(6)} %select_n.8, s32[]{:T(128)S(6)} %select_n.9, s32[4,2,32,16]{2,3,1,0:T(8,128)} %param.13), kind=kLoop, calls=%fused_computation.2 | loop fusion | bytes 16680 | tf_op jit(solution)/shard_map/dynamic_slice | solution.py:487
  13.1 0.1 copy.11
  13.2 0.1 reshape.11
  13.3 0.1 pad_dynamic-slice_fusion
  13.4 0.2 copy.12
  13.6 0.1 reshape.12
  13.7 0.1 concatenate.7.p_ref
  13.8 1.9 %matrices.1 = (bf16[128,144]{1,0:T(8,128)(2,1)S(1)}, bf16[4,256,256]{2,1,0:T(8,128)(2,1)S(1)}, bf16[4,256,256]{2,1,0:T(8,128)(2,1)S(1)}, bf16[4,256,256]{2,1,0:T...) custom-call(f32[180]{0:T(256)S(1)} %div.14.k_ref.refs_0_), custom_call_target="tpu_custom_call" | custom-call | flops 8000000 | bytes 4000000 | tf_op jit(solution)/shard_map/matrices/pallas_call | solution.py:131
  15.7 0.0 collective-permute-done.l_ref
  15.7 3.7 %collective-permute-done.1.r_ref = f32[256,256]{1,0:T(8,128)S(1)} collective-permute-done((f32[256,256]{1,0:T(8,128)S(1)}, f32[256,256]{1,0:T(8,128)S(1)}, u32[]{:S(2)}, u32[]{:S(2)}) %collective-permute-start.1) | collective-permute-done | bytes 262176 | tf_op jit(solution)/shard_map/ppermute | solution.py:481
  19.4 0.1 pack_rows.1
  19.5 11.4 %collective-permute-start.2 = (f32[216,256]{1,0:T(8,128)S(1)}, f32[216,256]{1,0:T(8,128)S(1)}, u32[]{:S(2)}, u32[]{:S(2)}) collective-permute-start(f32[216,256]{1,0:T(8,128)S(1)} %get-tuple-element.39), channel_id=1, source_target_pairs={{0,1},{1,2},{2,3},{3,4},{4,5},{5,6},{6,7},{7,8},{8,9},{9,10},{10,1... | collective-permute-start | bytes 663560 | tf_op jit(solution)/shard_map/ppermute | solution.py:477
  31.0 1.9 %collective-permute-start.3 = (f32[216,256]{1,0:T(8,128)S(1)}, f32[216,256]{1,0:T(8,128)S(1)}, u32[]{:S(2)}, u32[]{:S(2)}) collective-permute-start(f32[216,256]{1,0:T(8,128)S(1)} %get-tuple-element.42), channel_id=1, source_target_pairs={{1,0},{2,1},{3,2},{4,3},{5,4},{6,5},{7,6},{8,7},{9,8},{10,9},{11,1... | collective-permute-start | bytes 663560 | tf_op jit(solution)/shard_map/ppermute | solution.py:481
  32.9 6.5 %warp.1 = (f32[4,8,32,256]{3,2,1,0:T(8,128)S(1)}, f32[4,32,128]{2,1,0:T(8,128)S(1)}, f32[4,8,32,256]{3,2,1,0:T(8,128)S(1)}, f32[4,32,128]{2,1,0:T(8,128)S(1)}, f...) custom-call(s32[184]{0:T(256)S(1)} %concatenate.7.p_ref, f32[4,8,64,256]{3,2,1,0:T(8,128)S(1)} %copy-done.3, ...), custom_call_target="tpu_custom_call" | custom-call | flops 6000000000 | bytes 8000000 | tf_op jit(solution)/shard_map/warp/pallas_call | solution.py:312
  39.4 7.4 %collective-permute-done.3.refs_3_ = f32[216,256]{1,0:T(8,128)S(1)} collective-permute-done((f32[216,256]{1,0:T(8,128)S(1)}, f32[216,256]{1,0:T(8,128)S(1)}, u32[]{:S(2)}, u32[]{:S(2)}) %collective-permute-start.3) | collective-permute-done | bytes 221216 | tf_op jit(solution)/shard_map/ppermute | solution.py:481
  46.8 5.3 %shard_map.82 = (f32[8,24,256]{2,1,0:T(8,128)S(1)}, f32[8,24,256]{2,1,0:T(8,128)S(1)}) custom-call(f32[180]{0:T(256)S(1)} %div.14.k_ref.refs_0_, f32[8,64,256]{2,1,0:T(8,128)S(1)} %copy-done.1, f32[64,256]{1,0:T(8,128)S(1)} %get-tuple-element.36.refs_2_, f32[216,256]{1,0:T(8,128)S(1)} %collective-permute-done.3.refs_3_, ...), custom_call_target="tpu_custom_call" | custom-call | flops 4000000000 | bytes 8000000 | tf_op jit(solution)/shard_map/pallas_call | solution.py:454
  52.0 1.9 %collective-permute-start.4 = (f32[8,24,256]{2,1,0:T(8,128)S(1)}, f32[8,24,256]{2,1,0:T(8,128)S(1)}, u32[]{:S(2)}, u32[]{:S(2)}) collective-permute-start(f32[8,24,256]{2,1,0:T(8,128)S(1)} %get-tuple-element.56), channel_id=1, source_target_pairs={{0,1},{1,2},{2,3},{3,4},{4,5},{5,6},{6,7},{7,8},{8,9},{9,10},{10,1... | collective-permute-start | bytes 589832 | tf_op jit(solution)/shard_map/ppermute | solution.py:477
  53.9 0.0 collective-permute-done.2.refs_3_
  54.0 5.3 %shard_map.83 = (f32[8,24,256]{2,1,0:T(8,128)S(1)}, f32[8,24,256]{2,1,0:T(8,128)S(1)}) custom-call(f32[180]{0:T(256)S(1)} %div.14.k_ref.refs_0_, f32[8,64,256]{2,1,0:T(8,128)S(1)} %copy-done.1, f32[64,256]{1,0:T(8,128)S(1)} %get-tuple-element.36.refs_2_, f32[216,256]{1,0:T(8,128)S(1)} %collective-permute-done.2.refs_3_, ...), custom_call_target="tpu_custom_call" | custom-call | flops 4000000000 | bytes 8000000 | tf_op jit(solution)/shard_map/pallas_call | solution.py:454
  59.2 2.6 %collective-permute-start.5 = (f32[8,24,256]{2,1,0:T(8,128)S(1)}, f32[8,24,256]{2,1,0:T(8,128)S(1)}, u32[]{:S(2)}, u32[]{:S(2)}) collective-permute-start(f32[8,24,256]{2,1,0:T(8,128)S(1)} %get-tuple-element.58), channel_id=1, source_target_pairs={{1,0},{2,1},{3,2},{4,3},{5,4},{6,5},{7,6},{8,7},{9,8},{10,9},{11,1... | collective-permute-start | bytes 589832 | tf_op jit(solution)/shard_map/ppermute | solution.py:481
  61.8 5.3 %shard_map.84 = f32[8,48,256]{2,1,0:T(8,128)S(1)} custom-call(f32[180]{0:T(256)S(1)} %div.14.k_ref.refs_0_, f32[8,64,256]{2,1,0:T(8,128)S(1)} %copy-done.1, f32[64,256]{1,0:T(8,128)S(1)} %get-tuple-element.36.refs_2_, f32[4,8,32,256]{3,2,1,0:T(8,128)S(1)} %get-tuple-element.37.refs_3_, f32[4,32,128]{2,1,0:T(8,128)S(1)} %get-tuple-element.60.refs_4_, ...), custom_call_target="tpu_custom_call" | custom-call | flops 4000000000 | bytes 8000000 | tf_op jit(solution)/shard_map/pallas_call | solution.py:454
  67.1 5.1 %collective-permute-done.5 = f32[8,24,256]{2,1,0:T(8,128)S(1)} collective-permute-done((f32[8,24,256]{2,1,0:T(8,128)S(1)}, f32[8,24,256]{2,1,0:T(8,128)S(1)}, u32[]{:S(2)}, u32[]{:S(2)}) %collective-permute-start.5) | collective-permute-done | bytes 196640 | tf_op jit(solution)/shard_map/ppermute | solution.py:481
  72.3 0.0 collective-permute-done.4
  72.3 0.9 %multiply_multiply_fusion = f32[8,64,256]{2,1,0:T(8,128)} fusion(f32[8,64,256]{2,1,0:T(8,128)S(1)} %copy-done.1, f32[8,24,256]{2,1,0:T(8,128)S(1)} %add.34, f32[8,24,256]{2,1,0:T(8,128)S(1)} %add.32, f32[8,48,256]{2,1,0:T(8,128)S(1)} %shard_map.84), kind=kLoop, calls=%fused_computation | loop fusion | flops 524288 | bytes 1835008 | tf_op jit(solution)/shard_map/mul | solution.py:517
  (12 shorter events, 0.1 us)
Async XLA Ops:
  0.0 1.0 %copy-start = (f32[8,64,256]{2,1,0:T(8,128)S(1)}, f32[8,64,256]{2,1,0:T(8,128)}, u32[]{:S(2)}) copy-start(f32[8,64,256]{2,1,0:T(8,128)} %refs_1_.5) | copy-start | bytes 1572868
  1.0 1.6 %copy-start.2 = (f32[4,8,64,256]{3,2,1,0:T(8,128)S(1)}, f32[4,8,64,256]{3,2,1,0:T(8,128)}, u32[]{:S(2)}) copy-start(f32[4,8,64,256]{3,2,1,0:T(8,128)} %v_ref.3) | copy-start | bytes 6291460
  2.6 10.7 %copy-start.4 = (s32[4,3,32,16]{2,3,1,0:T(8,128)S(1)}, s32[4,3,32,16]{2,3,1,0:T(8,128)}, u32[]{:S(2)}) copy-start(s32[4,3,32,16]{2,3,1,0:T(8,128)} %param.14) | copy-start | bytes 73732
  2.6 11.1 %copy-start.5 = (s32[2]{0:T(128)S(1)}, s32[2]{0:T(128)}, u32[]{:S(2)}) copy-start(s32[2]{0:T(128)} %constant.22.clone) | copy-start | bytes 28
  2.6 16.7 %copy-start.1 = (f32[8,64,256]{2,1,0:T(8,128)S(1)}, f32[8,64,256]{2,1,0:T(8,128)}, u32[]{:S(2)}) copy-start(f32[8,64,256]{2,1,0:T(8,128)} %refs_1_.5) | copy-start | bytes 1572868
  2.6 30.3 %copy-start.3 = (f32[4,8,64,256]{3,2,1,0:T(8,128)S(1)}, f32[4,8,64,256]{3,2,1,0:T(8,128)}, u32[]{:S(2)}) copy-start(f32[4,8,64,256]{3,2,1,0:T(8,128)} %v_ref.3) | copy-start | bytes 6291460
  4.6 11.1 %collective-permute-start = (f32[256,256]{1,0:T(8,128)}, f32[256,256]{1,0:T(8,128)S(1)}, u32[]{:S(2)}, u32[]{:S(2)}) collective-permute-start(f32[256,256]{1,0:T(8,128)} %get-tuple-element.34), channel_id=1, source_target_pairs={{0,32},{32,64},{64,96},{96,128},{128,160},{160,192},{192,224},{224... | collective-permute-start | bytes 786440 | tf_op jit(solution)/shard_map/ppermute | solution.py:477
  8.5 10.9 %collective-permute-start.1 = (f32[256,256]{1,0:T(8,128)S(1)}, f32[256,256]{1,0:T(8,128)S(1)}, u32[]{:S(2)}, u32[]{:S(2)}) collective-permute-start(f32[256,256]{1,0:T(8,128)S(1)} %get-tuple-element.35), channel_id=1, source_target_pairs={{32,0},{64,32},{96,64},{128,96},{160,128},{192,160},{224,192},{256... | collective-permute-start | bytes 786440 | tf_op jit(solution)/shard_map/ppermute | solution.py:481
  19.5 34.4 %collective-permute-start.2 = (f32[216,256]{1,0:T(8,128)S(1)}, f32[216,256]{1,0:T(8,128)S(1)}, u32[]{:S(2)}, u32[]{:S(2)}) collective-permute-start(f32[216,256]{1,0:T(8,128)S(1)} %get-tuple-element.39), channel_id=1, source_target_pairs={{0,1},{1,2},{2,3},{3,4},{4,5},{5,6},{6,7},{7,8},{8,9},{9,10},{10,1... | collective-permute-start | bytes 663560 | tf_op jit(solution)/shard_map/ppermute | solution.py:477
  31.0 15.8 %collective-permute-start.3 = (f32[216,256]{1,0:T(8,128)S(1)}, f32[216,256]{1,0:T(8,128)S(1)}, u32[]{:S(2)}, u32[]{:S(2)}) collective-permute-start(f32[216,256]{1,0:T(8,128)S(1)} %get-tuple-element.42), channel_id=1, source_target_pairs={{1,0},{2,1},{3,2},{4,3},{5,4},{6,5},{7,6},{8,7},{9,8},{10,9},{11,1... | collective-permute-start | bytes 663560 | tf_op jit(solution)/shard_map/ppermute | solution.py:481
  52.0 20.2 %collective-permute-start.4 = (f32[8,24,256]{2,1,0:T(8,128)S(1)}, f32[8,24,256]{2,1,0:T(8,128)S(1)}, u32[]{:S(2)}, u32[]{:S(2)}) collective-permute-start(f32[8,24,256]{2,1,0:T(8,128)S(1)} %get-tuple-element.56), channel_id=1, source_target_pairs={{0,1},{1,2},{2,3},{3,4},{4,5},{5,6},{6,7},{7,8},{8,9},{9,10},{10,1... | collective-permute-start | bytes 589832 | tf_op jit(solution)/shard_map/ppermute | solution.py:477
  59.2 13.0 %collective-permute-start.5 = (f32[8,24,256]{2,1,0:T(8,128)S(1)}, f32[8,24,256]{2,1,0:T(8,128)S(1)}, u32[]{:S(2)}, u32[]{:S(2)}) collective-permute-start(f32[8,24,256]{2,1,0:T(8,128)S(1)} %get-tuple-element.58), channel_id=1, source_target_pairs={{1,0},{2,1},{3,2},{4,3},{5,4},{6,5},{7,6},{8,7},{9,8},{10,9},{11,1... | collective-permute-start | bytes 589832 | tf_op jit(solution)/shard_map/ppermute | solution.py:481

commit v4 on v3

--- a/solution.py
+++ b/solution.py
@@ -338,7 +338,7 @@
     refs = refs[12:]
     outs = 1 if mode == "inner" else 2
     out_refs, refs = refs[:outs], refs[outs:]
-    d, g_hi, g_lo, g_t, cen, q_hi, q_lo, q_t, x2 = refs
+    d, g_hi, g_lo, g_t, cen, q_t, x2 = refs
     lane = iota((NEAR, 128), 1)
     lane_out = iota((VIEWS * SET, 128), 1)
     for z in range(Z):
@@ -396,10 +396,10 @@
             dot(g_hi[v], f_lo[v]) + dot(g_t[v], f_t[v]))
         strip = dot(g_t[v], f_s[v])
         taps = [k_ref[2 * VIEWS * TAPS + v * TAPS + t] for t in range(TAPS)]
-        for rb in range(SET // 16):
+        for rb in range(SET // 8):
             for t in range(2):
                 cols = slice(t * 128, t * 128 + 128)
-                at = [slice(z * SET + rb * 16, z * SET + rb * 16 + 16) for z in range(Z)]
+                at = [slice(z * SET + rb * 8, z * SET + rb * 8 + 8) for z in range(Z)]
                 f = [cen[v, at[z], cols] for z in range(Z)]
                 ratio = []
                 for z in range(Z):
@@ -407,14 +407,12 @@
                     for y in range(1, Z):
                         total = total + taps[y - z + 7] * f[y]
                     total = jnp.where(total == 0.0, 1.0, total)
-                    ratio.append(w_ref[v, z, rb * 16 : rb * 16 + 16, cols] / total)
+                    ratio.append(w_ref[v, z, rb * 8 : rb * 8 + 8, cols] / total)
                 for z in range(Z):
                     total = taps[z + 7] * ratio[0]
                     for y in range(1, Z):
                         total = total + taps[z - y + 7] * ratio[y]
-                    high, low = split(total)
-                    q_hi[v, at[z], cols] = high
-                    q_lo[v, at[z], cols] = low
+                    cen[v, at[z], cols] = total
         strip = planes_to_lanes([strip[z * SET : (z + 1) * SET] for z in range(Z)])
         total = taps[7] * strip
         for y in range(1, Z):
@@ -429,8 +427,9 @@
             q_t[v, z * SET : (z + 1) * SET, :] = jnp.where(lanes < 16, turn(high, -16 * z), jnp.where(
                 lanes < 32, turn(low, 16 - 16 * z), jnp.where(
                     lanes < 48, turn(high, 32 - 16 * z), 0.0))).astype(BF16)
-        x = (dot(q_hi[v], b_hi[v]) + dot(q_lo[v], b_hi[v])) + (
-            dot(q_hi[v], b_lo[v]) + dot(q_t[v], b_t[v]))
+        q_hi, q_lo = split(cen[v])
+        x = (dot(q_hi, b_hi[v]) + dot(q_lo, b_hi[v])) + (
+            dot(q_hi, b_lo[v]) + dot(q_t[v], b_t[v]))
         high, low = split(x)
         for z in range(Z):
             x2[z, 0, v] = high[z * SET : (z + 1) * SET]
@@ -463,8 +462,6 @@
             pltpu.VMEM((VIEWS, rows, 256), BF16),
             pltpu.VMEM((VIEWS, rows, 256), BF16),
             pltpu.VMEM((VIEWS, rows, 256), F32),
-            pltpu.VMEM((VIEWS, rows, 256), BF16),
-            pltpu.VMEM((VIEWS, rows, 256), BF16),
             pltpu.VMEM((VIEWS, rows, 128), BF16),
             pltpu.VMEM((Z, 2, VIEWS, SET, COLS), BF16),
         ],
@@ -494,14 +491,15 @@
     params = jnp.concatenate(
         [neighbours(block_offsets, j, i), neighbours(sub_shifts, j, i), j[None], i[None],
          jnp.array([lax.axis_size("gy") - 1, lax.axis_size("gx") - 1], jnp.int32)])
-    first, last = pack_edges(estimate, views)
+    first, last = pack_edges(*(pltpu.with_memory_space_constraint(a, pltpu.HBM) for a in (estimate, views)))
     left, right = from_before(last, "gx"), from_after(first, "gx")
     ly, *x_mats, m_mat, n_mat = matrices(kernels)
     mats = (ly, *x_mats, m_mat, n_mat)
     first, last, sides = pack_rows(estimate, left, right)
     below = from_after(first, "gy")
+    w_t, s_t, w_i, s_i, w_b, s_b = warp(params, views, left, right)
+    last, s_t = lax.optimization_barrier((last, s_t))
     above = from_before(last, "gy")
-    w_t, s_t, w_i, s_i, w_b, s_b = warp(params, views, left, right)
     bottom, down = main("bottom", kernels, estimate, sides, below, w_b, s_b, *mats)
     from_above = from_before(down, "gy")
     s_t, bottom, down = lax.optimization_barrier((s_t, bottom, down))

time: 73.6 us -> 66.4 us (0.902)
  the two profiles are of different devices: /device:TPU:7 before, /device:TPU:159 now
where the time goes in v4:
time: 66.4 us; the launch traced here: 66.1 us
  Pallas kernels  28 us (42%)
  starting transfers between devices  25.3 us (38%)
  waiting for transfers between devices  8.98 us (14%)
  other arithmetic  1.83 us (3%)
  local copies, waits for them, and re-layouts  1.69 us (3%)
    pallas_call x3, Pallas kernels, main(): pl.pallas_call(functools.partial(main_kernel, part), out_shape=[jax.Shape...  15.4 us
    ppermute x3, starting transfers between devices, from_before(): lax.ppermute(value, axis, [(i, i + 1) for i in range(lax.axis_size(axis)...  14.1 us
    ppermute x3, starting transfers between devices, from_after(): lax.ppermute(value, axis, [(i + 1, i) for i in range(lax.axis_size(axis)...  11.2 us
    ppermute x3, waiting for transfers between devices, from_after(): lax.ppermute(value, axis, [(i + 1, i) for i in range(lax.axis_size(axis)...  8.97 us
    pallas_call x1, Pallas kernels, warp(): pl.pallas_call(warp_kernel, grid=(VIEWS,), out_shape=[w, s] * 3, in_specs...  6.5 us
    pallas_call x1, Pallas kernels, pack_edges(): pl.pallas_call(pack_edges_kernel, grid=(VIEWS,), out_shape=[out, out], in...  4.06 us
    pallas_call x1, Pallas kernels, matrices(): pl.pallas_call(matrices_kernel, out_shape=[jax.ShapeDtypeStruct(s, BF16)...  1.89 us
  transfers between devices with their start and end apart: 6, of which 2 were waited for; matrix products, arithmetic and copies ran while one was open for 4% of the time, Pallas kernels for 36%

profile of v4, /device:TPU:159, one launch (start us, length us, event | category | flops | bytes accessed | tf_op | source)
XLA Modules:
  0.0 66.1 jit_solution(14116642903942047873)
XLA Ops:
  0.0 0.0 copy-start.4
  0.0 0.0 copy-start.5
  0.1 4.1 %pack_edges.1 = (f32[256,256]{1,0:T(8,128)S(1)}, f32[256,256]{1,0:T(8,128)}) custom-call(f32[8,64,256]{2,1,0:T(8,128)} %refs_1_.5, f32[4,8,64,256]{3,2,1,0:T(8,128)} %v_ref.3), custom_call_target="tpu_custom_call" | custom-call | flops 1000000 | bytes 3200000 | tf_op jit(solution)/shard_map/pack_edges/pallas_call | solution.py:161
  4.1 3.9 %collective-permute-start = (f32[256,256]{1,0:T(8,128)}, f32[256,256]{1,0:T(8,128)S(1)}, u32[]{:S(2)}, u32[]{:S(2)}) collective-permute-start(f32[256,256]{1,0:T(8,128)} %get-tuple-element.36), channel_id=1, source_target_pairs={{0,32},{32,64},{64,96},{96,128},{128,160},{160,192},{192,224},{224... | collective-permute-start | bytes 786440 | tf_op jit(solution)/shard_map/ppermute | solution.py:474
  8.0 1.9 %collective-permute-start.1 = (f32[256,256]{1,0:T(8,128)S(1)}, f32[256,256]{1,0:T(8,128)S(1)}, u32[]{:S(2)}, u32[]{:S(2)}) collective-permute-start(f32[256,256]{1,0:T(8,128)S(1)} %get-tuple-element.37), channel_id=1, source_target_pairs={{32,0},{64,32},{96,64},{128,96},{160,128},{192,160},{224,192},{256... | collective-permute-start | bytes 786440 | tf_op jit(solution)/shard_map/ppermute | solution.py:478
  10.0 0.8 %fusion.1 = f32[12]{0:T(128)S(1)} fusion(f32[4,15]{1,0:T(4,128)S(1)} %copy-done.3, f32[4,15]{1,0:T(4,128)} %param.11, f32[4,15]{1,0:T(4,128)} %param.10), kind=kLoop, calls=%fused_computation.5 | loop fusion | flops 528 | bytes 768 | tf_op jit(solution)/shard_map/reduce_sum | solution.py:490
  10.8 0.1 fusion
  10.9 0.1 div.14.k_ref.refs_0_
  11.0 0.9 %pad_dynamic-slice_fusion.1 = s32[4,2,3,3]{2,3,1,0:T(4,128)S(1)} fusion(s32[]{:T(128)S(6)} %select_n.8, s32[]{:T(128)S(6)} %select_n.9, s32[4,2,32,16]{2,3,1,0:T(8,128)} %param.13), kind=kLoop, calls=%fused_computation.2 | loop fusion | bytes 16680 | tf_op jit(solution)/shard_map/dynamic_slice | solution.py:484
  11.8 0.1 copy.11
  12.0 0.1 reshape.11
  12.1 0.1 pad_dynamic-slice_fusion
  12.2 0.2 copy.12
  12.4 0.1 reshape.12
  12.5 0.1 concatenate.7.p_ref
  12.6 1.9 %matrices.1 = (bf16[128,144]{1,0:T(8,128)(2,1)S(1)}, bf16[4,256,256]{2,1,0:T(8,128)(2,1)S(1)}, bf16[4,256,256]{2,1,0:T(8,128)(2,1)S(1)}, bf16[4,256,256]{2,1,0:T...) custom-call(f32[180]{0:T(256)S(1)} %div.14.k_ref.refs_0_), custom_call_target="tpu_custom_call" | custom-call | flops 8000000 | bytes 4000000 | tf_op jit(solution)/shard_map/matrices/pallas_call | solution.py:131
  14.5 0.0 collective-permute-done.l_ref
  14.5 4.5 %collective-permute-done.1.r_ref = f32[256,256]{1,0:T(8,128)S(1)} collective-permute-done((f32[256,256]{1,0:T(8,128)S(1)}, f32[256,256]{1,0:T(8,128)S(1)}, u32[]{:S(2)}, u32[]{:S(2)}) %collective-permute-start.1) | collective-permute-done | bytes 262176 | tf_op jit(solution)/shard_map/ppermute | solution.py:478
  18.9 0.1 pack_rows.1
  19.1 3.7 %collective-permute-start.3 = (f32[216,256]{1,0:T(8,128)S(1)}, f32[216,256]{1,0:T(8,128)S(1)}, u32[]{:S(2)}, u32[]{:S(2)}) collective-permute-start(f32[216,256]{1,0:T(8,128)S(1)} %get-tuple-element.46), channel_id=1, source_target_pairs={{1,0},{2,1},{3,2},{4,3},{5,4},{6,5},{7,6},{8,7},{9,8},{10,9},{11,1... | collective-permute-start | bytes 663560 | tf_op jit(solution)/shard_map/ppermute | solution.py:478
  22.8 6.5 %warp.1 = (f32[4,8,32,256]{3,2,1,0:T(8,128)S(1)}, f32[4,32,128]{2,1,0:T(8,128)S(1)}, f32[4,8,32,256]{3,2,1,0:T(8,128)S(1)}, f32[4,32,128]{2,1,0:T(8,128)S(1)}, f...) custom-call(s32[184]{0:T(256)S(1)} %concatenate.7.p_ref, f32[4,8,64,256]{3,2,1,0:T(8,128)S(1)} %copy-done.1, ...), custom_call_target="tpu_custom_call" | custom-call | flops 6000000000 | bytes 8000000 | tf_op jit(solution)/shard_map/warp/pallas_call | solution.py:312
  29.3 7.8 %collective-permute-start.2 = (f32[216,256]{1,0:T(8,128)S(1)}, f32[216,256]{1,0:T(8,128)S(1)}, u32[]{:S(2)}, u32[]{:S(2)}) collective-permute-start(f32[216,256]{1,0:T(8,128)S(1)} %get-tuple-element.43), channel_id=1, source_target_pairs={{0,1},{1,2},{2,3},{3,4},{4,5},{5,6},{6,7},{7,8},{8,9},{9,10},{10,1... | collective-permute-start | bytes 663560 | tf_op jit(solution)/shard_map/ppermute | solution.py:474
  37.2 0.0 collective-permute-done.3.refs_3_
  37.2 5.1 %shard_map.82 = (f32[8,24,256]{2,1,0:T(8,128)S(1)}, f32[8,24,256]{2,1,0:T(8,128)S(1)}) custom-call(f32[180]{0:T(256)S(1)} %div.14.k_ref.refs_0_, f32[8,64,256]{2,1,0:T(8,128)S(1)} %copy-done, f32[64,256]{1,0:T(8,128)S(1)} %get-tuple-element.38.refs_2_, f32[216,256]{1,0:T(8,128)S(1)} %collective-permute-done.3.refs_3_, ...), custom_call_target="tpu_custom_call" | custom-call | flops 4000000000 | bytes 8000000 | tf_op jit(solution)/shard_map/pallas_call | solution.py:453
  42.3 2.4 %collective-permute-start.4 = (f32[8,24,256]{2,1,0:T(8,128)S(1)}, f32[8,24,256]{2,1,0:T(8,128)S(1)}, u32[]{:S(2)}, u32[]{:S(2)}) collective-permute-start(f32[8,24,256]{2,1,0:T(8,128)S(1)} %get-tuple-element.60), channel_id=1, source_target_pairs={{0,1},{1,2},{2,3},{3,4},{4,5},{5,6},{6,7},{7,8},{8,9},{9,10},{10,1... | collective-permute-start | bytes 589832 | tf_op jit(solution)/shard_map/ppermute | solution.py:474
  44.7 0.0 collective-permute-done.2.refs_3_
  44.7 5.1 %shard_map.83 = (f32[8,24,256]{2,1,0:T(8,128)S(1)}, f32[8,24,256]{2,1,0:T(8,128)S(1)}) custom-call(f32[180]{0:T(256)S(1)} %div.14.k_ref.refs_0_, f32[8,64,256]{2,1,0:T(8,128)S(1)} %copy-done, f32[64,256]{1,0:T(8,128)S(1)} %get-tuple-element.38.refs_2_, f32[216,256]{1,0:T(8,128)S(1)} %collective-permute-done.2.refs_3_, ...), custom_call_target="tpu_custom_call" | custom-call | flops 4000000000 | bytes 8000000 | tf_op jit(solution)/shard_map/pallas_call | solution.py:453
  49.9 5.6 %collective-permute-start.5 = (f32[8,24,256]{2,1,0:T(8,128)S(1)}, f32[8,24,256]{2,1,0:T(8,128)S(1)}, u32[]{:S(2)}, u32[]{:S(2)}) collective-permute-start(f32[8,24,256]{2,1,0:T(8,128)S(1)} %get-tuple-element.62), channel_id=1, source_target_pairs={{1,0},{2,1},{3,2},{4,3},{5,4},{6,5},{7,6},{8,7},{9,8},{10,9},{11,1... | collective-permute-start | bytes 589832 | tf_op jit(solution)/shard_map/ppermute | solution.py:478
  55.5 5.2 %shard_map.84 = f32[8,48,256]{2,1,0:T(8,128)S(1)} custom-call(f32[180]{0:T(256)S(1)} %div.14.k_ref.refs_0_, f32[8,64,256]{2,1,0:T(8,128)S(1)} %copy-done, f32[64,256]{1,0:T(8,128)S(1)} %get-tuple-element.38.refs_2_, f32[4,8,32,256]{3,2,1,0:T(8,128)S(1)} %get-tuple-element.39.refs_3_, f32[4,32,128]{2,1,0:T(8,128)S(1)} %get-tuple-element.64.refs_4_, ...), custom_call_target="tpu_custom_call" | custom-call | flops 4000000000 | bytes 8000000 | tf_op jit(solution)/shard_map/pallas_call | solution.py:453
  60.6 4.5 %collective-permute-done.5 = f32[8,24,256]{2,1,0:T(8,128)S(1)} collective-permute-done((f32[8,24,256]{2,1,0:T(8,128)S(1)}, f32[8,24,256]{2,1,0:T(8,128)S(1)}, u32[]{:S(2)}, u32[]{:S(2)}) %collective-permute-start.5) | collective-permute-done | bytes 196640 | tf_op jit(solution)/shard_map/ppermute | solution.py:478
  65.1 0.0 collective-permute-done.4
  65.2 0.9 %multiply_multiply_fusion = f32[8,64,256]{2,1,0:T(8,128)} fusion(f32[8,64,256]{2,1,0:T(8,128)S(1)} %copy-done, f32[8,24,256]{2,1,0:T(8,128)S(1)} %add.34, f32[8,24,256]{2,1,0:T(8,128)S(1)} %add.32, f32[8,48,256]{2,1,0:T(8,128)S(1)} %shard_map.84), kind=kLoop, calls=%fused_computation | loop fusion | flops 524288 | bytes 1835008 | tf_op jit(solution)/shard_map/mul | solution.py:515
  (14 shorter events, 0.1 us)
Async XLA Ops:
  0.0 12.5 %copy-start.6 = (s32[2]{0:T(128)S(1)}, s32[2]{0:T(128)}, u32[]{:S(2)}) copy-start(s32[2]{0:T(128)} %constant.22.clone) | copy-start | bytes 28
  0.0 18.9 %copy-start = (f32[8,64,256]{2,1,0:T(8,128)S(1)}, f32[8,64,256]{2,1,0:T(8,128)}, u32[]{:S(2)}) copy-start(f32[8,64,256]{2,1,0:T(8,128)} %refs_1_.5) | copy-start | bytes 1572868
  0.0 22.8 %copy-start.1 = (f32[4,8,64,256]{3,2,1,0:T(8,128)S(1)}, f32[4,8,64,256]{3,2,1,0:T(8,128)}, u32[]{:S(2)}) copy-start(f32[4,8,64,256]{3,2,1,0:T(8,128)} %v_ref.3) | copy-start | bytes 6291460
  0.0 9.9 %copy-start.3 = (f32[4,15]{1,0:T(4,128)S(1)}, f32[4,15]{1,0:T(4,128)}, u32[]{:S(2)}) copy-start(f32[4,15]{1,0:T(4,128)} %param.12) | copy-start | bytes 724
  0.0 10.8 %copy-start.4 = (f32[4,15]{1,0:T(4,128)S(1)}, f32[4,15]{1,0:T(4,128)}, u32[]{:S(2)}) copy-start(f32[4,15]{1,0:T(4,128)} %param.11) | copy-start | bytes 724
  0.0 10.8 %copy-start.5 = (f32[4,15]{1,0:T(4,128)S(1)}, f32[4,15]{1,0:T(4,128)}, u32[]{:S(2)}) copy-start(f32[4,15]{1,0:T(4,128)} %param.10) | copy-start | bytes 724
  0.0 12.0 %copy-start.2 = (s32[4,3,32,16]{2,3,1,0:T(8,128)S(1)}, s32[4,3,32,16]{2,3,1,0:T(8,128)}, u32[]{:S(2)}) copy-start(s32[4,3,32,16]{2,3,1,0:T(8,128)} %param.14) | copy-start | bytes 73732
  4.1 10.3 %collective-permute-start = (f32[256,256]{1,0:T(8,128)}, f32[256,256]{1,0:T(8,128)S(1)}, u32[]{:S(2)}, u32[]{:S(2)}) collective-permute-start(f32[256,256]{1,0:T(8,128)} %get-tuple-element.36), channel_id=1, source_target_pairs={{0,32},{32,64},{64,96},{96,128},{128,160},{160,192},{192,224},{224... | collective-permute-start | bytes 786440 | tf_op jit(solution)/shard_map/ppermute | solution.py:474
  8.0 10.9 %collective-permute-start.1 = (f32[256,256]{1,0:T(8,128)S(1)}, f32[256,256]{1,0:T(8,128)S(1)}, u32[]{:S(2)}, u32[]{:S(2)}) collective-permute-start(f32[256,256]{1,0:T(8,128)S(1)} %get-tuple-element.37), channel_id=1, source_target_pairs={{32,0},{64,32},{96,64},{128,96},{160,128},{192,160},{224,192},{256... | collective-permute-start | bytes 786440 | tf_op jit(solution)/shard_map/ppermute | solution.py:478
  19.1 18.1 %collective-permute-start.3 = (f32[216,256]{1,0:T(8,128)S(1)}, f32[216,256]{1,0:T(8,128)S(1)}, u32[]{:S(2)}, u32[]{:S(2)}) collective-permute-start(f32[216,256]{1,0:T(8,128)S(1)} %get-tuple-element.46), channel_id=1, source_target_pairs={{1,0},{2,1},{3,2},{4,3},{5,4},{6,5},{7,6},{8,7},{9,8},{10,9},{11,1... | collective-permute-start | bytes 663560 | tf_op jit(solution)/shard_map/ppermute | solution.py:478
  29.3 15.4 %collective-permute-start.2 = (f32[216,256]{1,0:T(8,128)S(1)}, f32[216,256]{1,0:T(8,128)S(1)}, u32[]{:S(2)}, u32[]{:S(2)}) collective-permute-start(f32[216,256]{1,0:T(8,128)S(1)} %get-tuple-element.43), channel_id=1, source_target_pairs={{0,1},{1,2},{2,3},{3,4},{4,5},{5,6},{6,7},{7,8},{8,9},{9,10},{10,1... | collective-permute-start | bytes 663560 | tf_op jit(solution)/shard_map/ppermute | solution.py:474
  42.3 22.8 %collective-permute-start.4 = (f32[8,24,256]{2,1,0:T(8,128)S(1)}, f32[8,24,256]{2,1,0:T(8,128)S(1)}, u32[]{:S(2)}, u32[]{:S(2)}) collective-permute-start(f32[8,24,256]{2,1,0:T(8,128)S(1)} %get-tuple-element.60), channel_id=1, source_target_pairs={{0,1},{1,2},{2,3},{3,4},{4,5},{5,6},{6,7},{7,8},{8,9},{9,10},{10,1... | collective-permute-start | bytes 589832 | tf_op jit(solution)/shard_map/ppermute | solution.py:474
  49.9 15.2 %collective-permute-start.5 = (f32[8,24,256]{2,1,0:T(8,128)S(1)}, f32[8,24,256]{2,1,0:T(8,128)S(1)}, u32[]{:S(2)}, u32[]{:S(2)}) collective-permute-start(f32[8,24,256]{2,1,0:T(8,128)S(1)} %get-tuple-element.62), channel_id=1, source_target_pairs={{1,0},{2,1},{3,2},{4,3},{5,4},{6,5},{7,6},{8,7},{9,8},{10,9},{11,1... | collective-permute-start | bytes 589832 | tf_op jit(solution)/shard_map/ppermute | solution.py:478
